TPU v7x, 128 devices: a whole 4x4x4 slice. The times are simulated.
128 devices in a mesh: group: 8 (over z, core), patch: 16 (over x, y).
Axes of the slice: x: 4, y: 4, z: 4, core: 2. Of those that a mesh axis runs over, the one named last changes fastest.
Arguments:
- node_latent: bfloat16 [40960, 512], P(('group', 'patch')), may hold values from -6 to 6
- fine_latent: bfloat16 [262144, 512], P(('group', 'patch')), may hold values from -6 to 6
- coarse_latent: bfloat16 [65536, 512], P(('group', 'patch')), may hold values from -6 to 6
- fine_sender: int32 [262144], P(('group', 'patch')), may hold values from 0 to 447
- fine_receiver: int32 [262144], P(('group', 'patch')), may hold values from 0 to 319
- coarse_owner: int32 [65536, 1], P(('group', 'patch')), may hold values from 0 to 127; in each aligned block of 512 rows (0 to 511, 512 to 1023, ...) at most 8 rows name the same one
- coarse_row: int32 [65536], P(('group', 'patch')), may hold values from 0 to 15
- coarse_receiver: int32 [65536], P(('group', 'patch')), may hold values from 0 to 15
- edge_first: bfloat16 [2, 1536, 512], replicated, may hold values from -0.15625 to 0.15625
- edge_bias: float32 [2, 512], replicated, may hold values from -3 to 3
- edge_second: bfloat16 [2, 512, 512], replicated, may hold values from -0.25 to 0.25
- edge_gain: float32 [2, 512], replicated, may hold values from 0.25 to 1.75
- node_first: bfloat16 [2, 1024, 512], replicated, may hold values from -0.1875 to 0.1875
- node_bias: float32 [2, 512], replicated, may hold values from -3 to 3
- node_second: bfloat16 [2, 512, 512], replicated, may hold values from -0.25 to 0.25
- node_gain: float32 [2, 512], replicated, may hold values from 0.25 to 1.75
Outputs:
- node_out: bfloat16 [40960, 512], P(('group', 'patch'))
- fine_out: bfloat16 [262144, 512], P(('group', 'patch'))
- coarse_out: bfloat16 [65536, 512], P(('group', 'patch'))
Inputs may be any that keep to these rules, and one draw needn't show every extreme that they name: `fine_sender`: A fine edge's sender indexes the receiving device's patch extended by 64 nodes on each side: values below 64 are the last 64 nodes of the previous patch of the same group, values from 384 on the first 64 nodes of the next patch; patches of a group close into a loop. `coarse_owner`: among the 512 coarse edges of one device, at most 8 have their sender on any one device.
All inputs are finite; a program needn't handle non-finite values.
Results may differ from a plain program's by a relative error of at most 0.0095.
Values may be sent and summed in bfloat16 or wider, within the bound.
A program may use at most 128 MiB of HBM per device.

v0:
```python
import jax
import jax.numpy as jnp
from jax import lax
from jax.sharding import PartitionSpec as P

HALO = 64
COARSE = 16
LAYERS = 2


EPSILON = 1e-05


def padded_2(block, sides, width):
    for axis, dim in sides:
        count = lax.axis_size(axis)
        forward = [(i, i + 1) for i in range(count - 1)]
        forward.append((count - 1, 0))
        backward = [(target, source) for source, target in forward]
        low = lax.ppermute(
            lax.slice_in_dim(block, block.shape[dim] - width, None, axis=dim), axis, forward
        )
        high = lax.ppermute(lax.slice_in_dim(block, 0, width, axis=dim), axis, backward)
        block = jnp.concatenate([low, block, high], axis=dim)
    return block


def norm_rows(values, gain_row):
    centre = jnp.mean(values, axis=-1, keepdims=True)
    centred = values - centre
    variance = jnp.mean(centred * centred, axis=-1, keepdims=True)
    return centred * lax.rsqrt(variance + EPSILON) * gain_row


def select_rows(selector, table):
    return jnp.dot(selector, table, preferred_element_type=jnp.float32).astype(jnp.bfloat16)


def edge_block(latent, endpoints, weight_edge, weight_pair, bias_row, weight_second, gain_row):
    from_ends = jnp.dot(endpoints, weight_pair, preferred_element_type=jnp.float32)
    pre = jnp.dot(latent, weight_edge, preferred_element_type=jnp.float32) + from_ends + bias_row
    hidden = jax.nn.silu(pre).astype(jnp.bfloat16)
    output = jnp.dot(hidden, weight_second, preferred_element_type=jnp.float32)
    message = norm_rows(output, gain_row)
    updated = (latent.astype(jnp.float32) + message).astype(jnp.bfloat16)
    return (updated, message.astype(jnp.bfloat16))


def body(
    node_latent,
    fine_latent,
    coarse_latent,
    fine_sender,
    fine_receiver,
    coarse_owner,
    coarse_row,
    coarse_receiver,
    edge_first,
    edge_bias,
    edge_second,
    edge_gain,
    node_first,
    node_bias,
    node_second,
    node_gain,
):
    width = node_latent.shape[1]
    node_count = node_latent.shape[0]
    devices = lax.axis_size(("group", "patch"))
    halo_rows = HALO
    coarse_nodes = COARSE
    owners = coarse_owner[:, 0]
    gathered_index = owners * coarse_nodes + coarse_row
    node_range = jnp.arange(node_count, dtype=jnp.int32)
    padded_range = jnp.arange(node_count + 2 * halo_rows, dtype=jnp.int32)
    fine_onehot = (node_range[:, None] == fine_receiver[None, :]).astype(jnp.bfloat16)
    coarse_onehot = (node_range[:, None] == coarse_receiver[None, :]).astype(jnp.bfloat16)
    fine_to_receiver = (fine_receiver[:, None] == node_range[None, :]).astype(jnp.bfloat16)
    coarse_to_receiver = (coarse_receiver[:, None] == node_range[None, :]).astype(jnp.bfloat16)
    fine_to_sender = (fine_sender[:, None] == padded_range[None, :]).astype(jnp.bfloat16)
    gathered_range = jnp.arange(devices * coarse_nodes, dtype=jnp.int32)
    coarse_to_sender = (gathered_index[:, None] == gathered_range[None, :]).astype(jnp.bfloat16)
    latent = node_latent
    fine_state = fine_latent
    coarse_state = coarse_latent
    for layer_index in range(LAYERS):
        first = edge_first[layer_index]
        weight_edge = first[:width]
        weight_pair = first[width:]
        bias_row = edge_bias[layer_index]
        weight_second = edge_second[layer_index]
        gain_row = edge_gain[layer_index]
        padded = padded_2(latent, (("patch", 0),), halo_rows)
        own_coarse = latent[:coarse_nodes]
        sender_table = lax.all_gather(own_coarse, ("group", "patch"), axis=0, tiled=True)
        fine_ends = jnp.concatenate(
            [select_rows(fine_to_sender, padded), select_rows(fine_to_receiver, latent)], axis=1
        )
        coarse_ends = jnp.concatenate(
            [select_rows(coarse_to_sender, sender_table), select_rows(coarse_to_receiver, latent)],
            axis=1,
        )
        fine_state, fine_message = edge_block(
            fine_state, fine_ends, weight_edge, weight_pair, bias_row, weight_second, gain_row
        )
        coarse_state, coarse_message = edge_block(
            coarse_state, coarse_ends, weight_edge, weight_pair, bias_row, weight_second, gain_row
        )
        summed = jnp.dot(fine_onehot, fine_message, preferred_element_type=jnp.float32) + jnp.dot(
            coarse_onehot, coarse_message, preferred_element_type=jnp.float32
        )
        summed = summed.astype(jnp.bfloat16)
        node_weights = node_first[layer_index]
        pre = (
            jnp.dot(latent, node_weights[:width], preferred_element_type=jnp.float32)
            + jnp.dot(summed, node_weights[width:], preferred_element_type=jnp.float32)
            + node_bias[layer_index]
        )
        hidden = jax.nn.silu(pre).astype(jnp.bfloat16)
        output = jnp.dot(hidden, node_second[layer_index], preferred_element_type=jnp.float32)
        latent = (latent.astype(jnp.float32) + norm_rows(output, node_gain[layer_index])).astype(
            jnp.bfloat16
        )
    return (latent, fine_state, coarse_state)


def solution(mesh):
    in_specs = (
        P(("group", "patch"), None),
        P(("group", "patch"), None),
        P(("group", "patch"), None),
        P(("group", "patch")),
        P(("group", "patch")),
        P(("group", "patch"), None),
        P(("group", "patch")),
        P(("group", "patch")),
        P(),
        P(),
        P(),
        P(),
        P(),
        P(),
        P(),
        P(),
    )
    out_specs = (
        P(("group", "patch"), None),
        P(("group", "patch"), None),
        P(("group", "patch"), None),
    )
    return jax.shard_map(body, mesh=mesh, in_specs=in_specs, out_specs=out_specs, check_vma=False)
```

profile of v0, /device:TPU:1, one launch (start us, length us, event | category | flops | bytes accessed | tf_op | source)
XLA Modules:
  0.0 181.6 jit_solution(11054618840922823359)
XLA Ops:
  11.8 3.7 %collective-permute-start.1 = (bf16[64,512]{1,0:T(8,128)(2,1)S(1)}, bf16[64,512]{1,0:T(8,128)(2,1)S(1)}, u32[]{:S(2)}, u32[]{:S(2)}) collective-permute-start(bf16[64,512]{1,0:T(8,128)(2,1)S(1)} %get-tuple-element.9), channel_id=1, source_target_pairs={{1,0},{2,1},{3,2},{4,3},{5,4},{6,5},{7,6},{8,7},{9,8},{10,9},{11,1... | collective-permute-start | bytes 196616 | tf_op jit(solution)/shard_map/ppermute | solution.py:23
  20.0 2.3 %fusion.106 = f32[320,512]{1,0:T(8,128)} fusion(bf16[320,512]{1,0:T(8,128)(2,1)} %param.16, bf16[2,1024,512]{2,1,0:T(8,128)(2,1)} %param.28), kind=kOutput, calls=%fused_computation.118 | convolution fusion | flops 167772160 | bytes 1507328 | tf_op jit(solution)/shard_map/dot_general | solution.py:115
  22.4 2.7 %fusion.102 = f32[512,512]{1,0:T(8,128)} fusion(bf16[512,512]{1,0:T(8,128)(2,1)} %param.18, bf16[2,1536,512]{2,1,0:T(8,128)(2,1)} %param.24), kind=kOutput, calls=%fused_computation.115 | convolution fusion | flops 268435456 | bytes 2097152 | tf_op jit(solution)/shard_map/dot_general | solution.py:41
  25.2 2.5 %fusion.18 = bf16[2048,512]{1,0:T(8,128)(2,1)} fusion(bf16[320,512]{1,0:T(8,128)(2,1)S(1)} %copy-done.7, s32[2048]{0:T(1024)S(1)} %copy-done.15), kind=kOutput, calls=%fused_computation.29 | convolution fusion | flops 672792576 | bytes 2433024 | tf_op jit(solution)/shard_map/dot_general | solution.py:36
  28.7 2.4 %copy.19 = bf16[2048,512]{0,1:T(8,128)(2,1)} copy(bf16[2048,512]{1,0:T(8,128)(2,1)S(1)} %copy-done.5) | data formatting | bytes 4194304 | tf_op args[1]
  33.0 5.6 %fusion = f32[2048,512]{1,0:T(8,128)} fusion(bf16[2048,512]{1,0:T(8,128)(2,1)S(1)} %copy-done.19, bf16[2048,512]{1,0:T(8,128)(2,1)S(1)} %fusion.16, bf16[2,1536,512]{2,1,0:T(8,128)(2,1)} %param.24), kind=kOutput, calls=%fused_computation | convolution fusion | flops 2155872256 | bytes 9437184 | tf_op jit(solution)/shard_map/dot_general | solution.py:40
  38.6 7.1 %fusion.174 = (f32[2048]{0:T(1024)S(1)}, f32[2048,512]{0,1:T(8,128)}) fusion(bf16[2,512,512]{2,1,0:T(8,128)(2,1)S(1)} %copy-done.13, f32[2048,512]{1,0:T(8,128)} %fusion, bf16[2048,512]{1,0:T(8,128)(2,1)S(1)} %copy-done.5, f32[512]{0:T(512)S(1)} %bitcast.116, bf16[2,1536,512]{2,1,0:T(8,128)(2,1)} %param.24), kind=kOutput, calls=%fused_computation.187 | convolution fusion | flops 2155870208 | bytes 11544576 | tf_op jit(solution)/shard_map/dot_general | solution.py:43
  45.7 2.8 %multiply_reduce_fusion.1 = f32[2048]{0:T(1024)S(1)} fusion(f32[2048,512]{0,1:T(8,128)} %get-tuple-element.19, f32[2048]{0:T(1024)S(1)} %broadcast_multiply_fusion.1), kind=kLoop, calls=%fused_computation.17 | loop fusion | flops 3143680 | bytes 4210688 | tf_op jit(solution)/shard_map/reduce_sum | solution.py:31
  52.3 28.3 %all-gather.3.cloned.1.call-done = bf16[2048,512]{1,0:T(8,128)(2,1)} async-done(((bf16[16,512]{1,0:T(8,128)(2,1)}), bf16[2048,512]{1,0:T(8,128)(2,1)}) %all-gather.3.cloned.1.call-update) | async-done | bytes 2097168 | tf_op jit(solution)/shard_map/all_gather | solution.py:95
  80.6 3.7 %fusion.42 = bf16[512,512]{1,0:T(8,128)(2,1)} fusion(bf16[2048,512]{1,0:T(8,128)(2,1)} %all-gather.3.cloned.1.call-done, s32[512]{0:T(512)S(1)} %add.176), kind=kOutput, calls=%fused_computation.56 | convolution fusion | flops 1075052544 | bytes 2623488 | tf_op jit(solution)/shard_map/dot_general | solution.py:36
  84.3 3.3 %fusion.177 = (f32[512]{0:T(512)S(1)}, f32[512,512]{0,1:T(8,128)S(1)}) fusion(bf16[2,512,512]{2,1,0:T(8,128)(2,1)} %param.26, f32[512,512]{1,0:T(8,128)} %fusion.102, bf16[2,1536,512]{2,1,0:T(8,128)(2,1)} %param.24, bf16[512,512]{1,0:T(8,128)(2,1)} %convolution_convert_fusion.1, bf16[512,512]{1,0:T(8,128)(2,1)} %fusion.42, f32[512]{0:T(512)S(1)} %bitcast.117), kind=kOutput, calls=%fused_computation.188 | convolution fusion | flops 809500160 | bytes 4722688 | tf_op jit(solution)/shard_map/dot_general | solution.py:43
  87.8 2.4 %multiply_convert_fusion.5 = bf16[320,512]{1,0:T(8,128)(2,1)S(1)} fusion(f32[320,512]{1,0:T(8,128)} %fusion.106, f32[320,512]{1,0:T(8,128)} %fusion.21, f32[512,512]{0,1:T(8,128)S(1)} %get-tuple-element.21, bf16[2,1024,512]{2,1,0:T(8,128)(2,1)} %param.28, f32[512]{0:T(512)S(1)} %bitcast.107, f32[512]{0:T(512)S(1)} %add_rsqrt_fusion.5, ...), kind=kOutput, calls=%fused_computation.98 | convolution fusion | flops 338231296 | bytes 3221504 | tf_op jit(solution)/shard_map/dot_general | solution.py:116
  93.7 2.5 %fusion.19 = bf16[2048,512]{1,0:T(8,128)(2,1)} fusion(bf16[320,512]{1,0:T(8,128)(2,1)S(1)} %add_convert_fusion.5, s32[2048]{0:T(1024)S(1)} %copy-done.15), kind=kOutput, calls=%fused_computation.30 | convolution fusion | flops 672792576 | bytes 2433024 | tf_op jit(solution)/shard_map/dot_general | solution.py:36
  97.5 2.5 %fusion.91 = f32[512,512]{1,0:T(8,128)} fusion(bf16[512,512]{0,1:T(8,128)(2,1)S(1)} %add_convert_fusion.3, bf16[2,1536,512]{2,1,0:T(8,128)(2,1)} %param.24), kind=kOutput, calls=%fused_computation.105 | convolution fusion | flops 268435456 | bytes 2097152 | tf_op jit(solution)/shard_map/dot_general | solution.py:41
  100.3 4.8 %collective-permute-start.3 = (bf16[64,512]{1,0:T(8,128)(2,1)S(1)}, bf16[64,512]{1,0:T(8,128)(2,1)S(1)}, u32[]{:S(2)}, u32[]{:S(2)}) collective-permute-start(bf16[64,512]{1,0:T(8,128)(2,1)S(1)} %get-tuple-element.7), channel_id=1, source_target_pairs={{1,0},{2,1},{3,2},{4,3},{5,4},{6,5},{7,6},{8,7},{9,8},{10,9},{11,1... | collective-permute-start | bytes 196616 | tf_op jit(solution)/shard_map/ppermute | solution.py:23
  110.2 5.5 %fusion.4 = f32[2048,512]{1,0:T(8,128)} fusion(bf16[2048,512]{1,0:T(8,128)(2,1)S(1)} %copy-done.18, bf16[2048,512]{1,0:T(8,128)(2,1)S(1)} %fusion.17, bf16[2,1536,512]{2,1,0:T(8,128)(2,1)} %param.24), kind=kOutput, calls=%fused_computation.4 | convolution fusion | flops 2155872256 | bytes 9437184 | tf_op jit(solution)/shard_map/dot_general | solution.py:40
  115.7 7.4 %fusion.183 = (f32[2048]{0:T(1024)S(1)}, f32[2048,512]{0,1:T(8,128)}) fusion(bf16[2,512,512]{2,1,0:T(8,128)(2,1)} %param.26, f32[2048,512]{1,0:T(8,128)} %fusion.4, bf16[2048,512]{0,1:T(8,128)(2,1)S(1)} %add_convert_fusion.1, f32[512]{0:T(512)S(1)} %bitcast.113, bf16[2,1536,512]{2,1,0:T(8,128)(2,1)} %param.24), kind=kOutput, calls=%fused_computation.190 | convolution fusion | flops 2155870208 | bytes 11544576 | tf_op jit(solution)/shard_map/dot_general | solution.py:43
  123.1 2.8 %multiply_reduce_fusion = f32[2048]{0:T(1024)S(1)} fusion(f32[2048,512]{0,1:T(8,128)} %get-tuple-element.25, f32[2048]{0:T(1024)S(1)} %broadcast_multiply_fusion), kind=kLoop, calls=%fused_computation.10 | loop fusion | flops 3143680 | bytes 4210688 | tf_op jit(solution)/shard_map/reduce_sum | solution.py:31
  126.5 2.4 %add_convert_fusion = bf16[2048,512]{0,1:T(8,128)(2,1)} fusion(bf16[2048,512]{0,1:T(8,128)(2,1)S(1)} %add_convert_fusion.1, f32[2048,512]{0,1:T(8,128)S(1)} %copy-done, f32[512]{0:T(512)S(1)} %bitcast.101, f32[2048]{0:T(1024)S(1)} %add_rsqrt_fusion, f32[2048]{0:T(1024)S(1)} %broadcast_multiply_fusion), kind=kLoop, calls=%fused_computation.8 | loop fusion | flops 6291456 | bytes 8407040 | tf_op jit(solution)/shard_map/convert_element_type | solution.py:45
  128.9 3.9 %copy.21 = bf16[2048,512]{1,0:T(8,128)(2,1)} copy(bf16[2048,512]{0,1:T(8,128)(2,1)} %add_convert_fusion) | data formatting | bytes 4194304
  132.9 4.1 %fusion.20 = f32[320,512]{1,0:T(8,128)} fusion(f32[2048,512]{0,1:T(8,128)} %get-tuple-element.25, f32[512]{0:T(512)S(1)} %bitcast.102, f32[2048]{0:T(1024)S(1)} %add_rsqrt_fusion, f32[2048]{0:T(1024)S(1)} %broadcast_multiply_fusion, s32[2048]{0:T(1024)S(1)} %copy-done.15), kind=kOutput, calls=%fused_computation.32 | convolution fusion | flops 675938304 | bytes 4876288 | tf_op jit(solution)/shard_map/dot_general | solution.py:109
  137.0 25.9 %all-gather.5.cloned.1.call-done = bf16[2048,512]{1,0:T(8,128)(2,1)} async-done(((bf16[16,512]{1,0:T(8,128)(2,1)}), bf16[2048,512]{1,0:T(8,128)(2,1)}) %all-gather.5.cloned.1.call-update) | async-done | bytes 2097168 | tf_op jit(solution)/shard_map/all_gather | solution.py:95
  163.0 3.7 %fusion.43 = bf16[512,512]{1,0:T(8,128)(2,1)} fusion(bf16[2048,512]{1,0:T(8,128)(2,1)} %all-gather.5.cloned.1.call-done, s32[512]{0:T(512)S(1)} %add.176), kind=kOutput, calls=%fused_computation.57 | convolution fusion | flops 1075052544 | bytes 2623488 | tf_op jit(solution)/shard_map/dot_general | solution.py:36
  166.6 2.8 %fusion.186 = (f32[512]{0:T(512)S(1)}, f32[512,512]{0,1:T(8,128)S(1)}) fusion(bf16[2,512,512]{2,1,0:T(8,128)(2,1)} %param.26, f32[512,512]{1,0:T(8,128)S(1)} %copy-done.9, bf16[2,1536,512]{2,1,0:T(8,128)(2,1)} %param.24, bf16[512,512]{1,0:T(8,128)(2,1)S(1)} %copy-done.17, bf16[512,512]{1,0:T(8,128)(2,1)} %fusion.43, f32[512]{0:T(512)S(1)} %bitcast.114), kind=kOutput, calls=%fused_computation.191 | convolution fusion | flops 809500160 | bytes 4722688 | tf_op jit(solution)/shard_map/dot_general | solution.py:43
  (92 shorter events, 31.9 us)
Async XLA Ops:
  7.2 18.0 %copy-start.7 = (bf16[320,512]{1,0:T(8,128)(2,1)S(1)}, bf16[320,512]{1,0:T(8,128)(2,1)}, u32[]{:S(2)}) copy-start(bf16[320,512]{1,0:T(8,128)(2,1)} %param.16) | copy-start | bytes 983044
  7.2 17.9 %copy-start.10 = (f32[2,512]{1,0:T(2,128)S(1)}, f32[2,512]{1,0:T(2,128)}, u32[]{:S(2)}) copy-start(f32[2,512]{1,0:T(2,128)} %param.31) | copy-start | bytes 12292
  7.2 18.0 %copy-start.15 = (s32[2048]{0:T(1024)S(1)}, s32[2048]{0:T(1024)}, u32[]{:S(2)}) copy-start(s32[2048]{0:T(1024)} %param.20) | copy-start | bytes 24580
  7.2 73.4 %all-gather.3.cloned.1.call-start = ((), (), s32[]{:S(2)}) async-start(), calls=%async_computation | async-start | bytes 2113536 | tf_op jit(solution)/shard_map/all_gather | solution.py:95
  8.6 154.3 %all-gather.5.cloned.1.call-start = ((), (), s32[]{:S(2)}) async-start(), calls=%async_computation.1 | async-start | bytes 2113536 | tf_op jit(solution)/shard_map/all_gather | solution.py:95
  9.6 21.6 %collective-permute-start = (bf16[64,512]{1,0:T(8,128)(2,1)S(1)}, bf16[64,512]{1,0:T(8,128)(2,1)S(1)}, u32[]{:S(2)}, u32[]{:S(2)}) collective-permute-start(bf16[64,512]{1,0:T(8,128)(2,1)S(1)} %get-tuple-element.8), channel_id=1, source_target_pairs={{0,1},{1,2},{2,3},{3,4},{4,5},{5,6},{6,7},{7,8},{8,9},{9,10},{10,1... | collective-permute-start | bytes 196616 | tf_op jit(solution)/shard_map/ppermute | solution.py:20
  11.8 19.4 %collective-permute-start.1 = (bf16[64,512]{1,0:T(8,128)(2,1)S(1)}, bf16[64,512]{1,0:T(8,128)(2,1)S(1)}, u32[]{:S(2)}, u32[]{:S(2)}) collective-permute-start(bf16[64,512]{1,0:T(8,128)(2,1)S(1)} %get-tuple-element.9), channel_id=1, source_target_pairs={{1,0},{2,1},{3,2},{4,3},{5,4},{6,5},{7,6},{8,7},{9,8},{10,9},{11,1... | collective-permute-start | bytes 196616 | tf_op jit(solution)/shard_map/ppermute | solution.py:23
  22.4 5.3 %copy-start.12 = (s32[512,1]{0,1:T(1,128)S(1)}, s32[512,1]{0,1:T(1,128)}, u32[]{:S(2)}) copy-start(s32[512,1]{0,1:T(1,128)} %param.21) | copy-start | bytes 6148
  22.4 5.3 %copy-start.6 = (bf16[512,512]{1,0:T(8,128)(2,1)S(1)}, bf16[512,512]{1,0:T(8,128)(2,1)}, u32[]{:S(2)}) copy-start(bf16[512,512]{1,0:T(8,128)(2,1)} %param.18) | copy-start | bytes 1572868
  25.1 3.6 %copy-start.5 = (bf16[2048,512]{1,0:T(8,128)(2,1)S(1)}, bf16[2048,512]{1,0:T(8,128)(2,1)}, u32[]{:S(2)}) copy-start(bf16[2048,512]{1,0:T(8,128)(2,1)} %param.17) | copy-start | bytes 6291460
  27.7 3.5 %copy-start.11 = (s32[512]{0:T(512)S(1)}, s32[512]{0:T(512)}, u32[]{:S(2)}) copy-start(s32[512]{0:T(512)} %param.22) | copy-start | bytes 6148
  27.7 3.5 %copy-start.14 = (s32[2048]{0:T(1024)S(1)}, s32[2048]{0:T(1024)}, u32[]{:S(2)}) copy-start(s32[2048]{0:T(1024)} %param.19) | copy-start | bytes 24580
  32.9 5.6 %copy-start.13 = (bf16[2,512,512]{2,1,0:T(8,128)(2,1)S(1)}, bf16[2,512,512]{2,1,0:T(8,128)(2,1)}, u32[]{:S(2)}) copy-start(bf16[2,512,512]{2,1,0:T(8,128)(2,1)} %param.26) | copy-start | bytes 3145732
  45.7 3.4 %copy-start.1 = (f32[2048,512]{0,1:T(8,128)S(1)}, f32[2048,512]{0,1:T(8,128)}, u32[]{:S(2)}) copy-start(f32[2048,512]{0,1:T(8,128)} %get-tuple-element.19) | copy-start | bytes 12582916
  48.5 2.6 %copy-start.2 = (bf16[2048,512]{0,1:T(8,128)(2,1)S(1)}, bf16[2048,512]{0,1:T(8,128)(2,1)}, u32[]{:S(2)}) copy-start(bf16[2048,512]{0,1:T(8,128)(2,1)} %copy.19) | copy-start | bytes 6291460
  84.3 3.5 %copy-start.16 = (s32[512]{0:T(512)S(1)}, s32[512]{0:T(512)}, u32[]{:S(2)}) copy-start(s32[512]{0:T(512)} %param.23) | copy-start | bytes 6148
  87.6 4.3 %copy-start.3 = (f32[512,512]{0,1:T(8,128)}, f32[512,512]{0,1:T(8,128)S(1)}, u32[]{:S(2)}) copy-start(f32[512,512]{0,1:T(8,128)S(1)} %get-tuple-element.21) | copy-start | bytes 3145732
  100.0 8.6 %collective-permute-start.2 = (bf16[64,512]{1,0:T(8,128)(2,1)S(1)}, bf16[64,512]{1,0:T(8,128)(2,1)S(1)}, u32[]{:S(2)}, u32[]{:S(2)}) collective-permute-start(bf16[64,512]{1,0:T(8,128)(2,1)S(1)} %get-tuple-element.6), channel_id=1, source_target_pairs={{0,1},{1,2},{2,3},{3,4},{4,5},{5,6},{6,7},{7,8},{8,9},{9,10},{10,1... | collective-permute-start | bytes 196616 | tf_op jit(solution)/shard_map/ppermute | solution.py:20
  100.3 8.3 %collective-permute-start.3 = (bf16[64,512]{1,0:T(8,128)(2,1)S(1)}, bf16[64,512]{1,0:T(8,128)(2,1)S(1)}, u32[]{:S(2)}, u32[]{:S(2)}) collective-permute-start(bf16[64,512]{1,0:T(8,128)(2,1)S(1)} %get-tuple-element.7), channel_id=1, source_target_pairs={{1,0},{2,1},{3,2},{4,3},{5,4},{6,5},{7,6},{8,7},{9,8},{10,9},{11,1... | collective-permute-start | bytes 196616 | tf_op jit(solution)/shard_map/ppermute | solution.py:23
  107.3 2.8 %copy-start.18 = (bf16[2048,512]{1,0:T(8,128)(2,1)S(1)}, bf16[2048,512]{1,0:T(8,128)(2,1)}, u32[]{:S(2)}) copy-start(bf16[2048,512]{1,0:T(8,128)(2,1)} %fusion.19) | copy-start | bytes 6291460
  123.1 3.4 %copy-start = (f32[2048,512]{0,1:T(8,128)S(1)}, f32[2048,512]{0,1:T(8,128)}, u32[]{:S(2)}) copy-start(f32[2048,512]{0,1:T(8,128)} %get-tuple-element.25) | copy-start | bytes 12582916
  137.0 29.6 %copy-start.9 = (f32[512,512]{1,0:T(8,128)S(1)}, f32[512,512]{1,0:T(8,128)}, u32[]{:S(2)}) copy-start(f32[512,512]{1,0:T(8,128)} %fusion.91) | copy-start | bytes 3145732
  137.0 29.6 %copy-start.17 = (bf16[512,512]{1,0:T(8,128)(2,1)S(1)}, bf16[512,512]{1,0:T(8,128)(2,1)}, u32[]{:S(2)}) copy-start(bf16[512,512]{1,0:T(8,128)(2,1)} %convolution_convert_fusion) | copy-start | bytes 1572868
  169.9 3.2 %copy-start.8 = (bf16[2,512,512]{2,1,0:T(8,128)(2,1)S(1)}, bf16[2,512,512]{2,1,0:T(8,128)(2,1)}, u32[]{:S(2)}) copy-start(bf16[2,512,512]{2,1,0:T(8,128)(2,1)} %param.30) | copy-start | bytes 3145732
  (2 other events, 4.3 us)
Sparse Core Ops, SparseCore 0:
  11.6 68.9 all-gather.2
  100.1 62.7 all-gather.4
where the time goes:
time: 182 us
  matrix products  73.3 us (40%)
  waiting for transfers between devices  54.3 us (30%)
  local copies, waits for them, and re-layouts  14.9 us (8%)
  between operations  14.3 us (8%)
  other arithmetic  13.7 us (8%)
  starting transfers between devices  11 us (6%)
    all_gather x2, waiting for transfers between devices, body(): lax.all_gather(own_coarse, ('group', 'patch'), axis=0, tiled=True)  54.3 us
    dot_general x4, matrix products, edge_block(): output = jnp.dot(hidden, weight_second, preferred_element_type=jnp.float32)  20.6 us
    dot_general x8, matrix products, select_rows(): jnp.dot(selector, table, preferred_element_type=jnp.float32)  19.2 us
    dot_general x2, matrix products, edge_block(): jnp.dot(endpoints, weight_pair, preferred_element_type=jnp.float32)  11.1 us
    unnamed x44, local copies, waits for them, and re-layouts  9.72 us
    ppermute x2, starting transfers between devices, padded_2(): lax.ppermute(lax.slice_in_dim(block, 0, width, axis=dim), axis, backward)  8.49 us
    reduce_sum x6, other arithmetic, norm_rows(): variance = jnp.mean(centred * centred, axis=-1, keepdims=True)  6.42 us
    dot_general x2, matrix products, body(): jnp.dot(fine_onehot, fine_message, preferred_element_type=jnp.float32)  6.12 us
  transfers between devices with their start and end apart: 6, of which 2 were waited for; matrix products, arithmetic and copies ran while one was open for 38% of the time, Pallas kernels for 0%

commit v1 on v0

v1 whole, which is shorter than its diff:
```python
import functools

import jax
import jax.numpy as jnp
from jax import lax
from jax.experimental import pallas as pl
from jax.experimental.pallas import tpu as pltpu
from jax.sharding import PartitionSpec as P

D = 512
NODE = 320
FINE = 2048
CE = 512
HALO = 64
COARSE = 16
LAYERS = 2
PAD = NODE + 2 * HALO
TABLE = PAD + NODE
GATHERED = 128 * COARSE
CHUNK = 256
CHUNKS = FINE // CHUNK
EPSILON = 1e-05
F32 = jnp.float32
BF16 = jnp.bfloat16


def mm(a, b):
    return jnp.dot(a, b, preferred_element_type=F32)


def silu_half(pre):
    u = pre * 0.5
    return (u + u * jnp.tanh(u)).astype(BF16)


def norm_rows(values, gain_row):
    centred = values - jnp.mean(values, axis=-1, keepdims=True)
    variance = jnp.mean(centred * centred, axis=-1, keepdims=True)
    return centred * lax.rsqrt(variance + EPSILON) * gain_row


def onehot(cond):
    return jnp.where(cond, 1.0, 0.0).astype(BF16)


def column(row):
    return jnp.transpose(jnp.broadcast_to(row, (128, 128)))


def kernel(
    h_hbm, fine_hbm, coarse_hbm, fs, fr, co, cr, cv, ef_hbm, eb, e2_hbm, eg, nf_hbm, nb, n2_hbm, ng,
    node_out, fine_out, coarse_out,
    L, ohT, CL, coh, crh, cohT, R, Wsr, W2, Nf, N2, H, halo, T, agg, pc, pn,
    lsem, fsem, osem, ssem, rsem,
    *, comm,
):
    loads = {
        "h": pltpu.make_async_copy(h_hbm, H.at[0], lsem.at[0]),
        "wsr0": pltpu.make_async_copy(ef_hbm.at[0, pl.ds(D, 2 * D)], Wsr.at[0], lsem.at[1]),
        "r0": pltpu.make_async_copy(ef_hbm.at[0, pl.ds(0, D)], R.at[0, pl.ds(0, D)], lsem.at[2]),
        "w2": pltpu.make_async_copy(e2_hbm, W2, lsem.at[3]),
        "nf": pltpu.make_async_copy(nf_hbm, Nf, lsem.at[4]),
        "coarse": pltpu.make_async_copy(coarse_hbm, CL, lsem.at[5]),
        "n2": pltpu.make_async_copy(n2_hbm, N2, lsem.at[6]),
        "wsr1": pltpu.make_async_copy(ef_hbm.at[1, pl.ds(D, 2 * D)], Wsr.at[1], lsem.at[7]),
        "r1": pltpu.make_async_copy(ef_hbm.at[1, pl.ds(0, D)], R.at[1, pl.ds(0, D)], lsem.at[8]),
    }

    def fine_load(i):
        rows = pl.ds(pl.multiple_of(i * CHUNK, CHUNK), CHUNK)
        return pltpu.make_async_copy(fine_hbm.at[rows], L.at[rows, pl.ds(0, D)], fsem.at[i])

    def fine_store(i):
        rows = pl.ds(pl.multiple_of(i * CHUNK, CHUNK), CHUNK)
        return pltpu.make_async_copy(L.at[rows, pl.ds(0, D)], fine_out.at[rows], fsem.at[CHUNKS + i])

    loads["h"].start()
    loads["wsr0"].start()
    loads["r0"].start()
    fine_load(0).start()
    fine_load(1).start()
    loads["w2"].start()
    for i in range(2, CHUNKS):
        fine_load(i).start()
    for name in ("coarse", "nf", "n2", "wsr1", "r1"):
        loads[name].start()

    if comm:
        group = lax.axis_index("group")
        patch = lax.axis_index("patch")
        z, c = group // 2, group % 2
        x, y = patch // 4, patch % 4
        i1 = (1 - c) * y + c * z
        i2 = (1 - c) * x + c * y
        i3 = (1 - c) * z + c * x

        def device(j1, j2, j3, core):
            jy = (1 - c) * j1 + c * j2
            jx = (1 - c) * j2 + c * j3
            jz = (1 - c) * j3 + c * j1
            return {"group": jz * 2 + core, "patch": jx * 4 + jy}

        def base(j1, j2, j3):
            return pl.multiple_of((((c * 4 + j3) * 4 + j2) * 4 + j1) * COARSE, COARSE)

        def turn(i, k):
            return (i + k) % 4

        stage1 = [device(turn(i1, k), i2, i3, c) for k in (1, 3, 2)]
        stage2 = [device(i1, turn(i2, k), i3, c) for k in (1, 3, 2)]
        right, left = (device(i1, i2, turn(i3, k), c) for k in (1, 3))
        partner = {"group": z * 2 + (1 - c), "patch": patch}
        following = {"group": group, "patch": (patch + 1) % 16}
        previous = {"group": group, "patch": (patch + 15) % 16}

        def remote(l, k, src, dst, target):
            return pltpu.make_async_remote_copy(
                src_ref=src, dst_ref=dst, send_sem=ssem.at[l, k], recv_sem=rsem.at[l, k],
                device_id=target, device_id_type=pl.DeviceIdType.MESH,
            )

        def same(l, k, start, count, target):
            ref = T.at[l, pl.ds(start, count)]
            return remote(l, k, ref, ref, target)

        def halos(l):
            return [
                remote(l, 0, H.at[l, pl.ds(NODE - HALO, HALO)], halo.at[l, pl.ds(0, HALO)], following),
                remote(l, 1, H.at[l, pl.ds(0, HALO)], halo.at[l, pl.ds(HALO, HALO)], previous),
            ]

        def own(l):
            return pltpu.make_async_copy(
                H.at[l, pl.ds(0, COARSE)], T.at[l, pl.ds(base(i1, i2, i3), COARSE)], osem.at[2 + l]
            )

        def gather1(l):
            return [
                remote(l, 2 + k, H.at[l, pl.ds(0, COARSE)], T.at[l, pl.ds(base(i1, i2, i3), COARSE)], to)
                for k, to in enumerate(stage1)
            ]

        def gather2(l):
            return [same(l, 5 + k, base(0, i2, i3), 4 * COARSE, to) for k, to in enumerate(stage2)]

        def gather3(l):
            half_a, half_b = base(0, 0, i3), base(0, 2, i3)
            return [
                same(l, 8, half_a, 128, right),
                same(l, 9, half_b, 128, left),
                same(l, 10, half_b, 128, right),
                same(l, 11, half_a, 128, left),
            ]

        def relays(l):
            return [
                same(l, 12, base(0, 0, turn(i3, 3)), 128, right),
                same(l, 13, base(0, 2, turn(i3, 1)), 128, left),
            ]

        def across(l):
            return [
                same(l, 14, base(0, 0, i3), 256, partner),
                same(l, 15, base(0, 0, turn(i3, 3)), 256, partner),
                same(l, 16, base(0, 0, turn(i3, 1)), 256, partner),
                same(l, 17, base(0, 0, turn(i3, 2)), 128, partner),
                same(l, 18, base(0, 2, turn(i3, 2)), 128, partner),
            ]

        barrier = pltpu.get_barrier_semaphore()
        peers = [*stage1, *stage2, right, left, partner, following, previous]
        for peer in peers:
            pl.semaphore_signal(barrier, inc=1, device_id=peer, device_id_type=pl.DeviceIdType.MESH)

        def begin(l):
            for copy in [*gather1(l), *halos(l), own(l)]:
                copy.start()

        def step1(l):
            for copy in gather1(l):
                copy.wait_recv()
            own(l).wait()
            for copy in gather2(l):
                copy.start()

        def step2(l):
            for copy in gather2(l):
                copy.wait_recv()
            for copy in [*gather3(l), across(l)[0]]:
                copy.start()

        def step3(l):
            sent = gather3(l)
            sent[0].wait_recv()
            relays(l)[0].start()
            sent[1].wait_recv()
            relays(l)[1].start()

        def step4(l):
            sent = gather3(l)
            sent[2].wait_recv()
            across(l)[1].start()
            sent[3].wait_recv()
            across(l)[2].start()

        def step5(l):
            for k in range(2):
                relays(l)[k].wait_recv()
                across(l)[3 + k].start()

        def finish(l):
            for copy in across(l):
                copy.wait_recv()
            for copy in [*halos(l), *gather1(l), *gather2(l), *gather3(l), *relays(l), *across(l)]:
                copy.wait_send()

        def wait_halos(l):
            for copy in halos(l):
                copy.wait_recv()
    else:
        begin = step1 = step2 = step3 = step4 = step5 = finish = wait_halos = lambda l: None

    lane = lax.broadcasted_iota(jnp.int32, (128, 128), 1)
    row_node = lax.broadcasted_iota(jnp.int32, (NODE, 128), 0)

    def build_fine(k, carry):
        sender = column(fs[pl.ds(k, 1), :])
        receiver_row = fr[pl.ds(k, 1), :]
        receiver = column(receiver_row) + PAD
        rows = pl.ds(pl.multiple_of(k * 128, 128), 128)
        for b in range(TABLE // 128):
            at = lane + b * 128
            if b < 3:
                cond = sender == at
            elif b == 3:
                cond = (sender == at) | (receiver == at)
            else:
                cond = receiver == at
            L[rows, D + b * 128 : D + (b + 1) * 128] = onehot(cond)
        ohT[:, rows] = onehot(row_node == receiver_row)
        return carry

    def build_coarse(k, carry):
        owner = co[pl.ds(k, 1), :]
        oz, oc, ox, oy = owner >> 5, (owner >> 4) & 1, (owner >> 2) & 3, owner & 3
        block0 = oz * 16 + ox * 4 + oy
        block1 = 64 + ox * 16 + oy * 4 + oz
        block = (1 - oc) * block0 + oc * block1
        sender = column(block * COARSE + cr[pl.ds(k, 1), :])
        receiver_row = cv[pl.ds(k, 1), :]
        rows = pl.ds(pl.multiple_of(k * 128, 128), 128)
        for b in range(GATHERED // 128):
            coh[rows, b * 128 : (b + 1) * 128] = onehot(sender == lane + b * 128)
        crh[rows, :] = onehot(column(receiver_row) == lane)
        cohT[:, rows] = onehot(lax.broadcasted_iota(jnp.int32, (COARSE, 128), 0) == receiver_row)
        return carry

    loads["h"].wait()
    if comm:
        pl.semaphore_wait(barrier, len(peers))
    begin(0)
    lax.fori_loop(0, FINE // 128, build_fine, 0)
    loads["wsr0"].wait()

    def fine_chunk(l, i):
        rows = pl.ds(pl.multiple_of(i * CHUNK, CHUNK), CHUNK)
        hidden = silu_half(mm(L[rows, :], R[l]))
        message = norm_rows(mm(hidden, W2[l]), eg[pl.ds(l, 1), :])
        L[rows, 0:D] = (L[rows, 0:D].astype(F32) + message).astype(BF16)
        agg[...] += mm(ohT[:, rows], message.astype(BF16))

    def layer(l, carry):
        latent = H[l]
        R[l, D + HALO : D + HALO + NODE] = mm(latent, Wsr[l, 0:D]).astype(BF16)
        R[l, D + PAD : D + TABLE] = (mm(latent, Wsr[l, D : 2 * D]) + eb[pl.ds(l, 1), :]).astype(BF16)
        agg[...] = jnp.zeros_like(agg)
        step1(l)
        wait_halos(l)
        ends = mm(halo[l], Wsr[l, 0:D]).astype(BF16)
        R[l, D : D + HALO] = ends[0:HALO]
        R[l, D + HALO + NODE : D + PAD] = ends[HALO : 2 * HALO]

        @pl.when(l == 0)
        def _():
            loads["r0"].wait()
            loads["w2"].wait()

        def chunk_step(i, inner):
            @pl.when(i == 2)
            def _():
                step2(l)

            @pl.when(i == 5)
            def _():
                step3(l)

            @pl.when(i == 7)
            def _():
                step4(l)

            @pl.when(l == 0)
            def _():
                fine_load(i).wait()

            fine_chunk(l, i)

            @pl.when(l == LAYERS - 1)
            def _():
                fine_store(i).start()

            return inner

        lax.fori_loop(0, CHUNKS, chunk_step, 0)

        @pl.when(l == 0)
        def _():
            lax.fori_loop(0, CE // 128, build_coarse, 0)
            for name in ("coarse", "nf", "n2", "wsr1", "r1"):
                loads[name].wait()

        pc[...] = mm(CL[...], R[l, 0:D]) + mm(crh[...], R[l, D + PAD : D + PAD + 128])
        step5(l)
        pn[...] = mm(latent, Nf[l, 0:D]) + nb[pl.ds(l, 1), :]
        finish(l)

        sender = mm(coh[...], T[l]).astype(BF16)
        hidden = silu_half(pc[...] + mm(sender, Wsr[l, 0:D]))
        message = norm_rows(mm(hidden, W2[l]), eg[pl.ds(l, 1), :])
        CL[...] = (CL[...].astype(F32) + message).astype(BF16)

        @pl.when(l == LAYERS - 1)
        def _():
            pltpu.make_async_copy(CL, coarse_out, osem.at[0]).start()

        agg[0:COARSE, :] += mm(cohT[...], message.astype(BF16))
        node_hidden = silu_half(pn[...] + mm(agg[...].astype(BF16), Nf[l, D : 2 * D]))
        update = norm_rows(mm(node_hidden, N2[l]), ng[pl.ds(l, 1), :])
        H[l + 1] = (latent.astype(F32) + update).astype(BF16)

        @pl.when(l < LAYERS - 1)
        def _():
            begin(l + 1)

        return carry

    lax.fori_loop(0, LAYERS, layer, 0)
    last = pltpu.make_async_copy(H.at[LAYERS], node_out, osem.at[1])
    last.start()
    for i in range(CHUNKS):
        fine_store(i).wait()
    pltpu.make_async_copy(CL, coarse_out, osem.at[0]).wait()
    last.wait()


def call(comm, *args):
    (node, fine, coarse, fs, fr, co, cr, cv, ef, eb, e2, eg, nf, nb, n2, ng) = args
    anyspec = pl.BlockSpec(memory_space=pl.ANY)
    vmem = pl.BlockSpec(memory_space=pltpu.VMEM)
    copies = 19
    return pl.pallas_call(
        functools.partial(kernel, comm=comm),
        name="processor",
        out_shape=(
            jax.ShapeDtypeStruct((NODE, D), BF16),
            jax.ShapeDtypeStruct((FINE, D), BF16),
            jax.ShapeDtypeStruct((CE, D), BF16),
        ),
        in_specs=[anyspec] * 3 + [vmem] * 5 + [anyspec, vmem, anyspec, vmem] * 2,
        out_specs=(anyspec, anyspec, anyspec),
        scratch_shapes=[
            pltpu.VMEM((FINE, D + TABLE), BF16),
            pltpu.VMEM((NODE, FINE), BF16),
            pltpu.VMEM((CE, D), BF16),
            pltpu.VMEM((CE, GATHERED), BF16),
            pltpu.VMEM((CE, 128), BF16),
            pltpu.VMEM((COARSE, CE), BF16),
            pltpu.VMEM((LAYERS, D + TABLE, D), BF16),
            pltpu.VMEM((LAYERS, 2 * D, D), BF16),
            pltpu.VMEM((LAYERS, D, D), BF16),
            pltpu.VMEM((LAYERS, 2 * D, D), BF16),
            pltpu.VMEM((LAYERS, D, D), BF16),
            pltpu.VMEM((LAYERS + 1, NODE, D), BF16),
            pltpu.VMEM((LAYERS, 2 * HALO, D), BF16),
            pltpu.VMEM((LAYERS, GATHERED, D), BF16),
            pltpu.VMEM((NODE, D), F32),
            pltpu.VMEM((CE, D), F32),
            pltpu.VMEM((NODE, D), F32),
            pltpu.SemaphoreType.DMA((9,)),
            pltpu.SemaphoreType.DMA((2 * CHUNKS,)),
            pltpu.SemaphoreType.DMA((4,)),
            pltpu.SemaphoreType.DMA((LAYERS, copies)),
            pltpu.SemaphoreType.DMA((LAYERS, copies)),
        ],
        compiler_params=pltpu.CompilerParams(
            collective_id=0 if comm else None, has_side_effects=True, vmem_limit_bytes=56 * 1024 * 1024
        ),
    )(
        node, fine, coarse,
        fs.reshape(FINE // 128, 128), fr.reshape(FINE // 128, 128),
        co.reshape(CE // 128, 128), cr.reshape(CE // 128, 128), cv.reshape(CE // 128, 128),
        ef, eb, e2, eg, nf, nb, n2, ng,
    )


def solution(mesh):
    rows = P(("group", "patch"), None)
    flat = P(("group", "patch"))
    in_specs = (rows, rows, rows, flat, flat, rows, flat, flat) + (P(),) * 8
    return jax.shard_map(
        functools.partial(call, True), mesh=mesh, in_specs=in_specs, out_specs=(rows, rows, rows), check_vma=False
    )
```

time: 182 us -> 61.9 us (0.34)
  matrix products: 73.3 us -> 0 us
  Pallas kernels: 0 us -> 55.5 us
  waiting for transfers between devices: 54.3 us -> 0 us
  other arithmetic: 13.7 us -> 0 us
  between operations: 14.3 us -> 0.65 us
  starting transfers between devices: 11 us -> 0 us
  local copies, waits for them, and re-layouts: 14.9 us -> 5.62 us
    dot_general x24 -> x0, matrix products: 73.3 us -> none  [the longest x4 20.6 us: edge_block(): output = jnp.dot(hidden, weight_second, preferred_element_type=jnp.float32)]
    pallas_call x0 -> x1, Pallas kernels: none -> 55.5 us  [call(): pl.pallas_call(functools.partial(kernel, comm=comm), name='processor', ou...]
    all_gather x2 -> x0, waiting for transfers between devices: 54.3 us -> none  [body(): lax.all_gather(own_coarse, ('group', 'patch'), axis=0, tiled=True)]
    ppermute x4 -> x0, starting transfers between devices: 11 us -> none  [the longest x2 8.49 us: padded_2(): lax.ppermute(lax.slice_in_dim(block, 0, width, axis=dim), axis, backward)]
    convert_element_type x6 -> x0, other arithmetic: 7.17 us -> none  [the longest x4 5.07 us: edge_block(): updated = (latent.astype(jnp.float32) + message).astype(jnp.bfloat16)]
    reduce_sum x6 -> x0, other arithmetic: 6.42 us -> none  [norm_rows(): variance = jnp.mean(centred * centred, axis=-1, keepdims=True)]
    slice x8 -> x0, local copies, waits for them, and re-layouts: 5.18 us -> none  [the longest x2 1.99 us: body(): own_coarse = latent[:coarse_nodes]]
    unnamed x44 -> x5, local copies, waits for them, and re-layouts: 9.72 us -> 5.62 us
  transfers between devices with their start and end apart: 6 -> 0, of which waited for: 2 -> 0; matrix products, arithmetic and copies ran while one was open for 38% -> 0% of each run, Pallas kernels for 0% -> 0%
where the time goes in v1:
time: 61.9 us; the launch traced here: 61.7 us
  Pallas kernels  55.5 us (90%)
  local copies, waits for them, and re-layouts  5.62 us (9%)
  between operations  0.65 us (1%)
    pallas_call x1, Pallas kernels, call(): pl.pallas_call(functools.partial(kernel, comm=comm), name='processor', ou...  55.5 us
    unnamed x5, local copies, waits for them, and re-layouts  5.62 us

profile of v1, /device:TPU:1, one launch (start us, length us, event | category | flops | bytes accessed | tf_op | source)
XLA Modules:
  0.0 61.7 jit_solution(14988927322531744179)
XLA Ops:
  0.6 55.5 %processor.1 = (bf16[320,512]{1,0:T(8,128)(2,1)}, bf16[2048,512]{1,0:T(8,128)(2,1)}, bf16[512,512]{1,0:T(8,128)(2,1)}) custom-call(bf16[320,512]{1,0:T(8,128)(2,1)} %h_hbm.1, bf16[2048,512]{1,0:T(8,128)(2,1)} %fine_hbm.1, bf16[512,512]{1,0:T(8,128)(2,1)} %coarse_hbm.1, s32[16,128]{1,0:T(8,128)} %bitcast.5, s32[16,128]{1,0:T(8,128)} %bitcast.6, ...), custom_call_target="tpu_custom_call" | custom-call | tf_op jit(solution)/shard_map/processor/pallas_call | solution.py:360
  56.1 1.7 %copy.22 = bf16[320,512]{1,0:T(8,128)(2,1)} copy(bf16[320,512]{1,0:T(8,128)(2,1)} %get-tuple-element.6) | data formatting | bytes 655360
  57.8 0.0 copy-start
  57.8 3.1 %copy.23 = bf16[2048,512]{1,0:T(8,128)(2,1)} copy(bf16[2048,512]{1,0:T(8,128)(2,1)} %get-tuple-element.7) | data formatting | bytes 4194304
  60.9 0.0 copy-done
  60.9 0.8 %copy.24 = bf16[512,512]{1,0:T(8,128)(2,1)} copy(bf16[512,512]{1,0:T(8,128)(2,1)S(1)} %copy-done) | data formatting | bytes 1048576
Async XLA Ops:
  57.8 3.1 %copy-start = (bf16[512,512]{1,0:T(8,128)(2,1)S(1)}, bf16[512,512]{1,0:T(8,128)(2,1)}, u32[]{:S(2)}) copy-start(bf16[512,512]{1,0:T(8,128)(2,1)} %get-tuple-element.8) | copy-start | bytes 1572868

commit v2 on v1

--- a/solution.py
+++ b/solution.py
@@ -17,7 +17,7 @@
 PAD = NODE + 2 * HALO
 TABLE = PAD + NODE
 GATHERED = 128 * COARSE
-CHUNK = 256
+CHUNK = 512
 CHUNKS = FINE // CHUNK
 EPSILON = 1e-05
 F32 = jnp.float32
@@ -90,28 +90,32 @@
         patch = lax.axis_index("patch")
         z, c = group // 2, group % 2
         x, y = patch // 4, patch % 4
-        i1 = (1 - c) * y + c * z
-        i2 = (1 - c) * x + c * y
-        i3 = (1 - c) * z + c * x
-
-        def device(j1, j2, j3, core):
-            jy = (1 - c) * j1 + c * j2
-            jx = (1 - c) * j2 + c * j3
-            jz = (1 - c) * j3 + c * j1
-            return {"group": jz * 2 + core, "patch": jx * 4 + jy}
-
-        def base(j1, j2, j3):
-            return pl.multiple_of((((c * 4 + j3) * 4 + j2) * 4 + j1) * COARSE, COARSE)
-
-        def turn(i, k):
-            return (i + k) % 4
-
-        stage1 = [device(turn(i1, k), i2, i3, c) for k in (1, 3, 2)]
-        stage2 = [device(i1, turn(i2, k), i3, c) for k in (1, 3, 2)]
-        right, left = (device(i1, i2, turn(i3, k), c) for k in (1, 3))
+        here = (x, y, z)
+
+        def swap1(i):
+            return i + 1 - 2 * (i % 2)
+
+        def swap3(i):
+            return 3 - i
+
+        def cube(swap):
+            targets = []
+            for mask in range(1, 8):
+                tx, ty, tz = (swap(i) if mask >> k & 1 else i for k, i in enumerate(here))
+                targets.append({"group": tz * 2 + c, "patch": tx * 4 + ty})
+            return targets
+
+        near, far = cube(swap1), cube(swap3)
+        first, second = (near, far), (far, near)
         partner = {"group": z * 2 + (1 - c), "patch": patch}
         following = {"group": group, "patch": (patch + 1) % 16}
         previous = {"group": group, "patch": (patch + 15) % 16}
+
+        def bundle(side):
+            pair = [(i + side) // 2 % 2 for i in here]
+            return ((c * 2 + side) * 8 + pair[0] * 4 + pair[1] * 2 + pair[2]) * 64
+
+        within = ((x % 2) * 4 + (y % 2) * 2 + z % 2) * 8
 
         def remote(l, k, src, dst, target):
             return pltpu.make_async_remote_copy(
@@ -120,7 +124,7 @@
             )
 
         def same(l, k, start, count, target):
-            ref = T.at[l, pl.ds(start, count)]
+            ref = T.at[l, pl.ds(pl.multiple_of(start, 8), count)]
             return remote(l, k, ref, ref, target)
 
         def halos(l):
@@ -129,96 +133,54 @@
                 remote(l, 1, H.at[l, pl.ds(0, HALO)], halo.at[l, pl.ds(HALO, HALO)], previous),
             ]
 
-        def own(l):
-            return pltpu.make_async_copy(
-                H.at[l, pl.ds(0, COARSE)], T.at[l, pl.ds(base(i1, i2, i3), COARSE)], osem.at[2 + l]
-            )
-
-        def gather1(l):
-            return [
-                remote(l, 2 + k, H.at[l, pl.ds(0, COARSE)], T.at[l, pl.ds(base(i1, i2, i3), COARSE)], to)
-                for k, to in enumerate(stage1)
-            ]
-
-        def gather2(l):
-            return [same(l, 5 + k, base(0, i2, i3), 4 * COARSE, to) for k, to in enumerate(stage2)]
-
-        def gather3(l):
-            half_a, half_b = base(0, 0, i3), base(0, 2, i3)
-            return [
-                same(l, 8, half_a, 128, right),
-                same(l, 9, half_b, 128, left),
-                same(l, 10, half_b, 128, right),
-                same(l, 11, half_a, 128, left),
-            ]
-
-        def relays(l):
-            return [
-                same(l, 12, base(0, 0, turn(i3, 3)), 128, right),
-                same(l, 13, base(0, 2, turn(i3, 1)), 128, left),
-            ]
-
-        def across(l):
-            return [
-                same(l, 14, base(0, 0, i3), 256, partner),
-                same(l, 15, base(0, 0, turn(i3, 3)), 256, partner),
-                same(l, 16, base(0, 0, turn(i3, 1)), 256, partner),
-                same(l, 17, base(0, 0, turn(i3, 2)), 128, partner),
-                same(l, 18, base(0, 2, turn(i3, 2)), 128, partner),
-            ]
+        def own(l, side):
+            dst = T.at[l, pl.ds(pl.multiple_of(bundle(side) + within, 8), 8)]
+            return H.at[l, pl.ds(side * 8, 8)], dst
+
+        def exchange(l):
+            return same(l, 4, c * 1024, 1024, partner)
 
         barrier = pltpu.get_barrier_semaphore()
-        peers = [*stage1, *stage2, right, left, partner, following, previous]
+        peers = [*near, *far, partner, following, previous]
         for peer in peers:
             pl.semaphore_signal(barrier, inc=1, device_id=peer, device_id_type=pl.DeviceIdType.MESH)
 
         def begin(l):
-            for copy in [*gather1(l), *halos(l), own(l)]:
+            for side in range(2):
+                for target in first[side]:
+                    remote(l, 2, *own(l, side), target).start()
+            for side in range(2):
+                pltpu.make_async_copy(*own(l, side), osem.at[2 + 2 * l + side]).start()
+            for copy in halos(l):
                 copy.start()
 
         def step1(l):
-            for copy in gather1(l):
-                copy.wait_recv()
-            own(l).wait()
-            for copy in gather2(l):
-                copy.start()
+            same(l, 2, 0, 14 * 8, partner).wait_recv()
+            for side in range(2):
+                pltpu.make_async_copy(*own(l, side), osem.at[2 + 2 * l + side]).wait()
+            for side in range(2):
+                for target in second[side]:
+                    same(l, 3, bundle(side), 64, target).start()
 
         def step2(l):
-            for copy in gather2(l):
-                copy.wait_recv()
-            for copy in [*gather3(l), across(l)[0]]:
-                copy.start()
-
-        def step3(l):
-            sent = gather3(l)
-            sent[0].wait_recv()
-            relays(l)[0].start()
-            sent[1].wait_recv()
-            relays(l)[1].start()
-
-        def step4(l):
-            sent = gather3(l)
-            sent[2].wait_recv()
-            across(l)[1].start()
-            sent[3].wait_recv()
-            across(l)[2].start()
-
-        def step5(l):
-            for k in range(2):
-                relays(l)[k].wait_recv()
-                across(l)[3 + k].start()
+            same(l, 3, 0, 14 * 64, partner).wait_recv()
+            exchange(l).start()
 
         def finish(l):
-            for copy in across(l):
-                copy.wait_recv()
-            for copy in [*halos(l), *gather1(l), *gather2(l), *gather3(l), *relays(l), *across(l)]:
+            exchange(l).wait_recv()
+
+        def drain(l):
+            same(l, 2, 0, 14 * 8, partner).wait_send()
+            same(l, 3, 0, 14 * 64, partner).wait_send()
+            for copy in [*halos(l), exchange(l)]:
                 copy.wait_send()
 
         def wait_halos(l):
             for copy in halos(l):
                 copy.wait_recv()
     else:
-        begin = step1 = step2 = step3 = step4 = step5 = finish = wait_halos = lambda l: None
+        c = 0
+        begin = step1 = step2 = finish = drain = wait_halos = lambda l: None
 
     lane = lax.broadcasted_iota(jnp.int32, (128, 128), 1)
     row_node = lax.broadcasted_iota(jnp.int32, (NODE, 128), 0)
@@ -242,11 +204,12 @@
 
     def build_coarse(k, carry):
         owner = co[pl.ds(k, 1), :]
+        row = cr[pl.ds(k, 1), :]
         oz, oc, ox, oy = owner >> 5, (owner >> 4) & 1, (owner >> 2) & 3, owner & 3
-        block0 = oz * 16 + ox * 4 + oy
-        block1 = 64 + ox * 16 + oy * 4 + oz
-        block = (1 - oc) * block0 + oc * block1
-        sender = column(block * COARSE + cr[pl.ds(k, 1), :])
+        side = row >> 3
+        px, py, pz = (((i + side) >> 1) & 1 for i in (ox, oy, oz))
+        place = ((px * 2 + py) * 2 + pz) * 8 + ((ox & 1) * 2 + (oy & 1)) * 2 + (oz & 1)
+        sender = column(((oc * 2 + side) * 64 + place) * 8 + (row & 7))
         receiver_row = cv[pl.ds(k, 1), :]
         rows = pl.ds(pl.multiple_of(k * 128, 128), 128)
         for b in range(GATHERED // 128):
@@ -269,16 +232,22 @@
         L[rows, 0:D] = (L[rows, 0:D].astype(F32) + message).astype(BF16)
         agg[...] += mm(ohT[:, rows], message.astype(BF16))
 
+    def node_rows(l, start, count, received):
+        rows = slice(start, start + count)
+        hidden = silu_half(pn[rows] + mm(received.astype(BF16), Nf[l, D : 2 * D]))
+        update = norm_rows(mm(hidden, N2[l]), ng[pl.ds(l, 1), :])
+        H[l + 1, rows] = (H[l, rows].astype(F32) + update).astype(BF16)
+
     def layer(l, carry):
         latent = H[l]
         R[l, D + HALO : D + HALO + NODE] = mm(latent, Wsr[l, 0:D]).astype(BF16)
         R[l, D + PAD : D + TABLE] = (mm(latent, Wsr[l, D : 2 * D]) + eb[pl.ds(l, 1), :]).astype(BF16)
         agg[...] = jnp.zeros_like(agg)
-        step1(l)
         wait_halos(l)
         ends = mm(halo[l], Wsr[l, 0:D]).astype(BF16)
         R[l, D : D + HALO] = ends[0:HALO]
         R[l, D + HALO + NODE : D + PAD] = ends[HALO : 2 * HALO]
+        step1(l)
 
         @pl.when(l == 0)
         def _():
@@ -286,18 +255,6 @@
             loads["w2"].wait()
 
         def chunk_step(i, inner):
-            @pl.when(i == 2)
-            def _():
-                step2(l)
-
-            @pl.when(i == 5)
-            def _():
-                step3(l)
-
-            @pl.when(i == 7)
-            def _():
-                step4(l)
-
             @pl.when(l == 0)
             def _():
                 fine_load(i).wait()
@@ -319,45 +276,61 @@
                 loads[name].wait()
 
         pc[...] = mm(CL[...], R[l, 0:D]) + mm(crh[...], R[l, D + PAD : D + PAD + 128])
-        step5(l)
         pn[...] = mm(latent, Nf[l, 0:D]) + nb[pl.ds(l, 1), :]
+        node_rows(l, COARSE, NODE - COARSE, agg[COARSE:NODE])
+        step2(l)
+        mine = pl.ds(pl.multiple_of(c * 1024, 1024), 1024)
+        other = pl.ds(pl.multiple_of((1 - c) * 1024, 1024), 1024)
+        sender = mm(coh[:, mine], T[l, mine])
         finish(l)
-
-        sender = mm(coh[...], T[l]).astype(BF16)
+        sender = (sender + mm(coh[:, other], T[l, other])).astype(BF16)
         hidden = silu_half(pc[...] + mm(sender, Wsr[l, 0:D]))
         message = norm_rows(mm(hidden, W2[l]), eg[pl.ds(l, 1), :])
-        CL[...] = (CL[...].astype(F32) + message).astype(BF16)
-
-        @pl.when(l == LAYERS - 1)
-        def _():
-            pltpu.make_async_copy(CL, coarse_out, osem.at[0]).start()
-
-        agg[0:COARSE, :] += mm(cohT[...], message.astype(BF16))
-        node_hidden = silu_half(pn[...] + mm(agg[...].astype(BF16), Nf[l, D : 2 * D]))
-        update = norm_rows(mm(node_hidden, N2[l]), ng[pl.ds(l, 1), :])
-        H[l + 1] = (latent.astype(F32) + update).astype(BF16)
+        node_rows(l, 0, COARSE, agg[0:COARSE] + mm(cohT[...], message.astype(BF16)))
 
         @pl.when(l < LAYERS - 1)
         def _():
             begin(l + 1)
 
+        CL[...] = (CL[...].astype(F32) + message).astype(BF16)
+        drain(l)
         return carry
 
     lax.fori_loop(0, LAYERS, layer, 0)
-    last = pltpu.make_async_copy(H.at[LAYERS], node_out, osem.at[1])
-    last.start()
+    finals = [
+        pltpu.make_async_copy(CL, coarse_out, osem.at[0]),
+        pltpu.make_async_copy(H.at[LAYERS], node_out, osem.at[1]),
+    ]
+    for copy in finals:
+        copy.start()
     for i in range(CHUNKS):
         fine_store(i).wait()
-    pltpu.make_async_copy(CL, coarse_out, osem.at[0]).wait()
-    last.wait()
+    for copy in finals:
+        copy.wait()
+
+
+def hand_over(node, fine, coarse, node_out, fine_out, coarse_out, N, F, C, sem):
+    pieces = [(coarse, C, coarse_out, 0, CE), (node, N, node_out, 0, NODE)]
+    pieces += [(fine, F, fine_out, k * 512, 512) for k in range(FINE // 512)]
+    arrive, leave = [], []
+    for k, (src, buffer, dst, start, count) in enumerate(pieces):
+        rows = pl.ds(start, count)
+        arrive.append(pltpu.make_async_copy(src.at[rows], buffer.at[rows], sem.at[0, k]))
+        leave.append(pltpu.make_async_copy(buffer.at[rows], dst.at[rows], sem.at[1, k]))
+        arrive[k].start()
+    for k in range(len(pieces)):
+        arrive[k].wait()
+        leave[k].start()
+    for copy in leave:
+        copy.wait()
 
 
 def call(comm, *args):
     (node, fine, coarse, fs, fr, co, cr, cv, ef, eb, e2, eg, nf, nb, n2, ng) = args
     anyspec = pl.BlockSpec(memory_space=pl.ANY)
     vmem = pl.BlockSpec(memory_space=pltpu.VMEM)
-    copies = 19
-    return pl.pallas_call(
+    copies = 5
+    results = pl.pallas_call(
         functools.partial(kernel, comm=comm),
         name="processor",
         out_shape=(
@@ -387,7 +360,7 @@
             pltpu.VMEM((NODE, D), F32),
             pltpu.SemaphoreType.DMA((9,)),
             pltpu.SemaphoreType.DMA((2 * CHUNKS,)),
-            pltpu.SemaphoreType.DMA((4,)),
+            pltpu.SemaphoreType.DMA((6,)),
             pltpu.SemaphoreType.DMA((LAYERS, copies)),
             pltpu.SemaphoreType.DMA((LAYERS, copies)),
         ],
@@ -400,6 +373,14 @@
         co.reshape(CE // 128, 128), cr.reshape(CE // 128, 128), cv.reshape(CE // 128, 128),
         ef, eb, e2, eg, nf, nb, n2, ng,
     )
+    return pl.pallas_call(
+        hand_over,
+        name="hand_over",
+        out_shape=tuple(jax.ShapeDtypeStruct((n, D), BF16) for n in (NODE, FINE, CE)),
+        in_specs=[anyspec] * 3,
+        out_specs=(anyspec,) * 3,
+        scratch_shapes=[pltpu.VMEM((n, D), BF16) for n in (NODE, FINE, CE)] + [pltpu.SemaphoreType.DMA((2, 6))],
+    )(*results)
 
 
 def solution(mesh):

time: 61.9 us -> 54.4 us (0.88)
  local copies, waits for them, and re-layouts: 5.62 us -> 0 us
  Pallas kernels: 55.5 us -> 53.6 us
    unnamed x5 -> x0, local copies, waits for them, and re-layouts: 5.62 us -> none
    pallas_call x1, Pallas kernels: 55.5 us -> 50.8 us  [call(): pl.pallas_call(functools.partial(kernel, comm=comm), name='processor', ou...]
    pallas_call x0 -> x1, Pallas kernels: none -> 2.74 us  [call(): pl.pallas_call(hand_over, name='hand_over', out_shape=tuple((jax.ShapeDty...]
where the time goes in v2:
time: 54.4 us; the launch traced here: 54.2 us
  Pallas kernels  53.6 us (99%)
  between operations  0.65 us (1%)
    pallas_call x1, Pallas kernels, call(): pl.pallas_call(functools.partial(kernel, comm=comm), name='processor', ou...  50.8 us
    pallas_call x1, Pallas kernels, call(): pl.pallas_call(hand_over, name='hand_over', out_shape=tuple((jax.ShapeDty...  2.74 us

profile of v2, /device:TPU:1, one launch (start us, length us, event | category | flops | bytes accessed | tf_op | source)
XLA Modules:
  0.0 54.2 jit_solution(8425969719833737739)
XLA Ops:
  0.6 50.8 %processor.1 = (bf16[320,512]{1,0:T(8,128)(2,1)}, bf16[2048,512]{1,0:T(8,128)(2,1)}, bf16[512,512]{1,0:T(8,128)(2,1)}) custom-call(bf16[320,512]{1,0:T(8,128)(2,1)} %h_hbm.1, bf16[2048,512]{1,0:T(8,128)(2,1)} %fine_hbm.1, bf16[512,512]{1,0:T(8,128)(2,1)} %coarse_hbm.1, s32[16,128]{1,0:T(8,128)} %bitcast.5, s32[16,128]{1,0:T(8,128)} %bitcast.6, ...), custom_call_target="tpu_custom_call" | custom-call | tf_op jit(solution)/shard_map/processor/pallas_call | solution.py:333
  51.5 2.7 %hand_over.1 = (bf16[320,512]{1,0:T(8,128)(2,1)}, bf16[2048,512]{1,0:T(8,128)(2,1)}, bf16[512,512]{1,0:T(8,128)(2,1)}) custom-call(bf16[320,512]{1,0:T(8,128)(2,1)} %get-tuple-element.6.node, bf16[2048,512]{1,0:T(8,128)(2,1)} %get-tuple-element.7.fine, bf16[512,512]{1,0:T(8,128)(2,1)} %get-tuple-element.8.coarse), custom_call_target="tpu_custom_call" | custom-call | tf_op jit(solution)/shard_map/hand_over/pallas_call | solution.py:376

commit v3 on v2

--- a/solution.py
+++ b/solution.py
@@ -29,8 +29,8 @@
 
 
 def silu_half(pre):
-    u = pre * 0.5
-    return (u + u * jnp.tanh(u)).astype(BF16)
+    u = (pre * 0.5).astype(BF16)
+    return u + u * jnp.tanh(u)
 
 
 def norm_rows(values, gain_row):
@@ -48,23 +48,35 @@
 
 
 def kernel(
-    h_hbm, fine_hbm, coarse_hbm, fs, fr, co, cr, cv, ef_hbm, eb, e2_hbm, eg, nf_hbm, nb, n2_hbm, ng,
+    h_hbm, fine_hbm, coarse_hbm, fs_hbm, fr_hbm, co_hbm, cr_hbm, cv_hbm,
+    ef_hbm, eb_hbm, e2_hbm, eg_hbm, nf_hbm, nb_hbm, n2_hbm, ng_hbm,
     node_out, fine_out, coarse_out,
     L, ohT, CL, coh, crh, cohT, R, Wsr, W2, Nf, N2, H, halo, T, agg, pc, pn,
+    fs, fr, co, cr, cv, eb, eg, nb, ng,
     lsem, fsem, osem, ssem, rsem,
     *, comm,
 ):
-    loads = {
-        "h": pltpu.make_async_copy(h_hbm, H.at[0], lsem.at[0]),
-        "wsr0": pltpu.make_async_copy(ef_hbm.at[0, pl.ds(D, 2 * D)], Wsr.at[0], lsem.at[1]),
-        "r0": pltpu.make_async_copy(ef_hbm.at[0, pl.ds(0, D)], R.at[0, pl.ds(0, D)], lsem.at[2]),
-        "w2": pltpu.make_async_copy(e2_hbm, W2, lsem.at[3]),
-        "nf": pltpu.make_async_copy(nf_hbm, Nf, lsem.at[4]),
-        "coarse": pltpu.make_async_copy(coarse_hbm, CL, lsem.at[5]),
-        "n2": pltpu.make_async_copy(n2_hbm, N2, lsem.at[6]),
-        "wsr1": pltpu.make_async_copy(ef_hbm.at[1, pl.ds(D, 2 * D)], Wsr.at[1], lsem.at[7]),
-        "r1": pltpu.make_async_copy(ef_hbm.at[1, pl.ds(0, D)], R.at[1, pl.ds(0, D)], lsem.at[8]),
-    }
+    plan = [
+        ("fs", fs_hbm, fs),
+        ("fr", fr_hbm, fr),
+        ("h", h_hbm, H.at[0]),
+        ("wsr0", ef_hbm.at[0, pl.ds(D, 2 * D)], Wsr.at[0]),
+        ("eb", eb_hbm, eb),
+        ("r0", ef_hbm.at[0, pl.ds(0, D)], R.at[0, pl.ds(0, D)]),
+        ("w2", e2_hbm, W2),
+        ("eg", eg_hbm, eg),
+        ("co", co_hbm, co),
+        ("cr", cr_hbm, cr),
+        ("cv", cv_hbm, cv),
+        ("nf", nf_hbm, Nf),
+        ("nb", nb_hbm, nb),
+        ("coarse", coarse_hbm, CL),
+        ("n2", n2_hbm, N2),
+        ("ng", ng_hbm, ng),
+        ("wsr1", ef_hbm.at[1, pl.ds(D, 2 * D)], Wsr.at[1]),
+        ("r1", ef_hbm.at[1, pl.ds(0, D)], R.at[1, pl.ds(0, D)]),
+    ]
+    loads = {name: pltpu.make_async_copy(src, dst, lsem.at[k]) for k, (name, src, dst) in enumerate(plan)}
 
     def fine_load(i):
         rows = pl.ds(pl.multiple_of(i * CHUNK, CHUNK), CHUNK)
@@ -74,16 +86,16 @@
         rows = pl.ds(pl.multiple_of(i * CHUNK, CHUNK), CHUNK)
         return pltpu.make_async_copy(L.at[rows, pl.ds(0, D)], fine_out.at[rows], fsem.at[CHUNKS + i])
 
-    loads["h"].start()
-    loads["wsr0"].start()
-    loads["r0"].start()
-    fine_load(0).start()
-    fine_load(1).start()
-    loads["w2"].start()
-    for i in range(2, CHUNKS):
-        fine_load(i).start()
-    for name in ("coarse", "nf", "n2", "wsr1", "r1"):
-        loads[name].start()
+    def start_loads():
+        for name, _, _ in plan[:6]:
+            loads[name].start()
+        fine_load(0).start()
+        loads["w2"].start()
+        loads["eg"].start()
+        for i in range(1, CHUNKS):
+            fine_load(i).start()
+        for name, _, _ in plan[8:]:
+            loads[name].start()
 
     if comm:
         group = lax.axis_index("group")
@@ -98,15 +110,17 @@
         def swap3(i):
             return 3 - i
 
-        def cube(swap):
+        def cube(swap, order):
             targets = []
-            for mask in range(1, 8):
+            for mask in order:
                 tx, ty, tz = (swap(i) if mask >> k & 1 else i for k, i in enumerate(here))
                 targets.append({"group": tz * 2 + c, "patch": tx * 4 + ty})
             return targets
 
-        near, far = cube(swap1), cube(swap3)
-        first, second = (near, far), (far, near)
+        swaps = (swap1, swap3)
+        stages = ((4,), (6, 2), (7, 5, 3, 1))
+        first = [[cube(swaps[side], masks) for masks in stages] for side in range(2)]
+        second = [cube(swaps[1 - side], (7, 6, 5, 3, 4, 2, 1)) for side in range(2)]
         partner = {"group": z * 2 + (1 - c), "patch": patch}
         following = {"group": group, "patch": (patch + 1) % 16}
         previous = {"group": group, "patch": (patch + 15) % 16}
@@ -115,7 +129,13 @@
             pair = [(i + side) // 2 % 2 for i in here]
             return ((c * 2 + side) * 8 + pair[0] * 4 + pair[1] * 2 + pair[2]) * 64
 
-        within = ((x % 2) * 4 + (y % 2) * 2 + z % 2) * 8
+        wx, wy, wz = (i % 2 for i in here)
+        within = (wx * 4 + wy * 2 + wz) * 8
+        pieces = (
+            ((wx * 4 + wy * 2) * 8, 16),
+            ((wx * 4 + (1 - wy) * 2) * 8, 16),
+            ((1 - wx) * 32, 32),
+        )
 
         def remote(l, k, src, dst, target):
             return pltpu.make_async_remote_copy(
@@ -127,60 +147,65 @@
             ref = T.at[l, pl.ds(pl.multiple_of(start, 8), count)]
             return remote(l, k, ref, ref, target)
 
-        def halos(l):
+        def halos(l, source):
             return [
-                remote(l, 0, H.at[l, pl.ds(NODE - HALO, HALO)], halo.at[l, pl.ds(0, HALO)], following),
-                remote(l, 1, H.at[l, pl.ds(0, HALO)], halo.at[l, pl.ds(HALO, HALO)], previous),
+                remote(l, 0, source.at[pl.ds(NODE - HALO, HALO)], halo.at[l, pl.ds(0, HALO)], following),
+                remote(l, 1, source.at[pl.ds(0, HALO)], halo.at[l, pl.ds(HALO, HALO)], previous),
             ]
 
-        def own(l, side):
+        def own(l, side, source):
             dst = T.at[l, pl.ds(pl.multiple_of(bundle(side) + within, 8), 8)]
-            return H.at[l, pl.ds(side * 8, 8)], dst
+            return source.at[pl.ds(side * 8, 8)], dst
 
         def exchange(l):
-            return same(l, 4, c * 1024, 1024, partner)
+            return same(l, 8, c * 1024, 1024, partner)
 
         barrier = pltpu.get_barrier_semaphore()
-        peers = [*near, *far, partner, following, previous]
+        peers = [*second[0], *second[1], partner, following, previous]
         for peer in peers:
             pl.semaphore_signal(barrier, inc=1, device_id=peer, device_id_type=pl.DeviceIdType.MESH)
 
-        def begin(l):
+        def begin(l, source):
+            for k in range(3):
+                for side in range(2):
+                    for target in first[side][k]:
+                        remote(l, 2 + k, *own(l, side, source), target).start()
             for side in range(2):
-                for target in first[side]:
-                    remote(l, 2, *own(l, side), target).start()
-            for side in range(2):
-                pltpu.make_async_copy(*own(l, side), osem.at[2 + 2 * l + side]).start()
-            for copy in halos(l):
+                pltpu.make_async_copy(*own(l, side, source), osem.at[2 + 2 * l + side]).start()
+            for copy in halos(l, source):
                 copy.start()
 
-        def step1(l):
-            same(l, 2, 0, 14 * 8, partner).wait_recv()
-            for side in range(2):
-                pltpu.make_async_copy(*own(l, side), osem.at[2 + 2 * l + side]).wait()
-            for side in range(2):
-                for target in second[side]:
-                    same(l, 3, bundle(side), 64, target).start()
+        def step1(l, k):
+            same(l, 2 + k, 0, 2 * len(stages[k]) * 8, partner).wait_recv()
+            if k == 0:
+                for side in range(2):
+                    pltpu.make_async_copy(*own(l, side, H.at[l]), osem.at[2 + 2 * l + side]).wait()
+            start, count = pieces[k]
+            for t in range(7):
+                for side in range(2):
+                    same(l, 5 + k, bundle(side) + start, count, second[side][t]).start()
 
         def step2(l):
-            same(l, 3, 0, 14 * 64, partner).wait_recv()
+            for k in range(3):
+                same(l, 5 + k, 0, 14 * pieces[k][1], partner).wait_recv()
             exchange(l).start()
 
         def finish(l):
             exchange(l).wait_recv()
 
         def drain(l):
-            same(l, 2, 0, 14 * 8, partner).wait_send()
-            same(l, 3, 0, 14 * 64, partner).wait_send()
-            for copy in [*halos(l), exchange(l)]:
+            for k in range(3):
+                same(l, 2 + k, 0, 2 * len(stages[k]) * 8, partner).wait_send()
+                same(l, 5 + k, 0, 14 * pieces[k][1], partner).wait_send()
+            for copy in [*halos(l, H.at[l]), exchange(l)]:
                 copy.wait_send()
 
         def wait_halos(l):
-            for copy in halos(l):
+            for copy in halos(l, H.at[l]):
                 copy.wait_recv()
     else:
         c = 0
-        begin = step1 = step2 = finish = drain = wait_halos = lambda l: None
+        begin = step1 = step2 = finish = drain = wait_halos = lambda *a: None
 
     lane = lax.broadcasted_iota(jnp.int32, (128, 128), 1)
     row_node = lax.broadcasted_iota(jnp.int32, (NODE, 128), 0)
@@ -218,19 +243,22 @@
         cohT[:, rows] = onehot(lax.broadcasted_iota(jnp.int32, (COARSE, 128), 0) == receiver_row)
         return carry
 
-    loads["h"].wait()
+    start_loads()
     if comm:
         pl.semaphore_wait(barrier, len(peers))
-    begin(0)
+    begin(0, h_hbm)
+    for name in ("fs", "fr"):
+        loads[name].wait()
     lax.fori_loop(0, FINE // 128, build_fine, 0)
-    loads["wsr0"].wait()
+    for name in ("h", "wsr0", "eb"):
+        loads[name].wait()
 
     def fine_chunk(l, i):
         rows = pl.ds(pl.multiple_of(i * CHUNK, CHUNK), CHUNK)
         hidden = silu_half(mm(L[rows, :], R[l]))
-        message = norm_rows(mm(hidden, W2[l]), eg[pl.ds(l, 1), :])
-        L[rows, 0:D] = (L[rows, 0:D].astype(F32) + message).astype(BF16)
-        agg[...] += mm(ohT[:, rows], message.astype(BF16))
+        message = norm_rows(mm(hidden, W2[l]), eg[pl.ds(l, 1), :]).astype(BF16)
+        L[rows, 0:D] += message
+        agg[...] += mm(ohT[:, rows], message)
 
     def node_rows(l, start, count, received):
         rows = slice(start, start + count)
@@ -243,16 +271,18 @@
         R[l, D + HALO : D + HALO + NODE] = mm(latent, Wsr[l, 0:D]).astype(BF16)
         R[l, D + PAD : D + TABLE] = (mm(latent, Wsr[l, D : 2 * D]) + eb[pl.ds(l, 1), :]).astype(BF16)
         agg[...] = jnp.zeros_like(agg)
+        step1(l, 0)
+        step1(l, 1)
         wait_halos(l)
         ends = mm(halo[l], Wsr[l, 0:D]).astype(BF16)
         R[l, D : D + HALO] = ends[0:HALO]
         R[l, D + HALO + NODE : D + PAD] = ends[HALO : 2 * HALO]
-        step1(l)
+        step1(l, 2)
 
         @pl.when(l == 0)
         def _():
-            loads["r0"].wait()
-            loads["w2"].wait()
+            for name in ("r0", "w2", "eg"):
+                loads[name].wait()
 
         def chunk_step(i, inner):
             @pl.when(l == 0)
@@ -268,31 +298,31 @@
             return inner
 
         lax.fori_loop(0, CHUNKS, chunk_step, 0)
+        step2(l)
 
         @pl.when(l == 0)
         def _():
+            for name in ("co", "cr", "cv", "nf", "nb", "coarse", "n2", "ng", "wsr1", "r1"):
+                loads[name].wait()
             lax.fori_loop(0, CE // 128, build_coarse, 0)
-            for name in ("coarse", "nf", "n2", "wsr1", "r1"):
-                loads[name].wait()
 
         pc[...] = mm(CL[...], R[l, 0:D]) + mm(crh[...], R[l, D + PAD : D + PAD + 128])
         pn[...] = mm(latent, Nf[l, 0:D]) + nb[pl.ds(l, 1), :]
         node_rows(l, COARSE, NODE - COARSE, agg[COARSE:NODE])
-        step2(l)
         mine = pl.ds(pl.multiple_of(c * 1024, 1024), 1024)
         other = pl.ds(pl.multiple_of((1 - c) * 1024, 1024), 1024)
         sender = mm(coh[:, mine], T[l, mine])
         finish(l)
         sender = (sender + mm(coh[:, other], T[l, other])).astype(BF16)
         hidden = silu_half(pc[...] + mm(sender, Wsr[l, 0:D]))
-        message = norm_rows(mm(hidden, W2[l]), eg[pl.ds(l, 1), :])
-        node_rows(l, 0, COARSE, agg[0:COARSE] + mm(cohT[...], message.astype(BF16)))
+        message = norm_rows(mm(hidden, W2[l]), eg[pl.ds(l, 1), :]).astype(BF16)
+        node_rows(l, 0, COARSE, agg[0:COARSE] + mm(cohT[...], message))
 
         @pl.when(l < LAYERS - 1)
         def _():
-            begin(l + 1)
-
-        CL[...] = (CL[...].astype(F32) + message).astype(BF16)
+            begin(l + 1, H.at[l + 1])
+
+        CL[...] += message
         drain(l)
         return carry
 
@@ -328,8 +358,7 @@
 def call(comm, *args):
     (node, fine, coarse, fs, fr, co, cr, cv, ef, eb, e2, eg, nf, nb, n2, ng) = args
     anyspec = pl.BlockSpec(memory_space=pl.ANY)
-    vmem = pl.BlockSpec(memory_space=pltpu.VMEM)
-    copies = 5
+    copies = 9
     results = pl.pallas_call(
         functools.partial(kernel, comm=comm),
         name="processor",
@@ -338,7 +367,7 @@
             jax.ShapeDtypeStruct((FINE, D), BF16),
             jax.ShapeDtypeStruct((CE, D), BF16),
         ),
-        in_specs=[anyspec] * 3 + [vmem] * 5 + [anyspec, vmem, anyspec, vmem] * 2,
+        in_specs=[anyspec] * 16,
         out_specs=(anyspec, anyspec, anyspec),
         scratch_shapes=[
             pltpu.VMEM((FINE, D + TABLE), BF16),
@@ -358,7 +387,16 @@
             pltpu.VMEM((NODE, D), F32),
             pltpu.VMEM((CE, D), F32),
             pltpu.VMEM((NODE, D), F32),
-            pltpu.SemaphoreType.DMA((9,)),
+            pltpu.VMEM((FINE // 128, 128), jnp.int32),
+            pltpu.VMEM((FINE // 128, 128), jnp.int32),
+            pltpu.VMEM((CE // 128, 128), jnp.int32),
+            pltpu.VMEM((CE // 128, 128), jnp.int32),
+            pltpu.VMEM((CE // 128, 128), jnp.int32),
+            pltpu.VMEM((LAYERS, D), F32),
+            pltpu.VMEM((LAYERS, D), F32),
+            pltpu.VMEM((LAYERS, D), F32),
+            pltpu.VMEM((LAYERS, D), F32),
+            pltpu.SemaphoreType.DMA((18,)),
             pltpu.SemaphoreType.DMA((2 * CHUNKS,)),
             pltpu.SemaphoreType.DMA((6,)),
             pltpu.SemaphoreType.DMA((LAYERS, copies)),

time: 54.4 us -> 50.6 us (0.930)
  Pallas kernels: 53.6 us -> 49.8 us
    pallas_call x1, Pallas kernels: 50.8 us -> 47.1 us  [call(): pl.pallas_call(functools.partial(kernel, comm=comm), name='processor', ou...]
where the time goes in v3:
time: 50.6 us; the launch traced here: 50.4 us
  Pallas kernels  49.8 us (98%)
  between operations  0.65 us (1%)
    pallas_call x1, Pallas kernels, call(): pl.pallas_call(functools.partial(kernel, comm=comm), name='processor', ou...  47.1 us
    pallas_call x1, Pallas kernels, call(): pl.pallas_call(hand_over, name='hand_over', out_shape=tuple((jax.ShapeDty...  2.74 us

profile of v3, /device:TPU:1, one launch (start us, length us, event | category | flops | bytes accessed | tf_op | source)
XLA Modules:
  0.0 50.4 jit_solution(6325727348822193954)
XLA Ops:
  0.6 47.1 %processor.1 = (bf16[320,512]{1,0:T(8,128)(2,1)}, bf16[2048,512]{1,0:T(8,128)(2,1)}, bf16[512,512]{1,0:T(8,128)(2,1)}) custom-call(bf16[320,512]{1,0:T(8,128)(2,1)} %h_hbm.1, bf16[2048,512]{1,0:T(8,128)(2,1)} %fine_hbm.1, bf16[512,512]{1,0:T(8,128)(2,1)} %coarse_hbm.1, s32[16,128]{1,0:T(8,128)} %bitcast.5, s32[16,128]{1,0:T(8,128)} %bitcast.6, ...), custom_call_target="tpu_custom_call" | custom-call | tf_op jit(solution)/shard_map/processor/pallas_call | solution.py:362
  47.7 2.7 %hand_over.1 = (bf16[320,512]{1,0:T(8,128)(2,1)}, bf16[2048,512]{1,0:T(8,128)(2,1)}, bf16[512,512]{1,0:T(8,128)(2,1)}) custom-call(bf16[320,512]{1,0:T(8,128)(2,1)} %get-tuple-element.6.node, bf16[2048,512]{1,0:T(8,128)(2,1)} %get-tuple-element.7.fine, bf16[512,512]{1,0:T(8,128)(2,1)} %get-tuple-element.8.coarse), custom_call_target="tpu_custom_call" | custom-call | tf_op jit(solution)/shard_map/hand_over/pallas_call | solution.py:414

commit v4 on v3

--- a/solution.py
+++ b/solution.py
@@ -17,8 +17,9 @@
 PAD = NODE + 2 * HALO
 TABLE = PAD + NODE
 GATHERED = 128 * COARSE
-CHUNK = 512
+CHUNK = 2048
 CHUNKS = FINE // CHUNK
+COARSE_CHUNK = 512
 EPSILON = 1e-05
 F32 = jnp.float32
 BF16 = jnp.bfloat16
@@ -51,7 +52,7 @@
     h_hbm, fine_hbm, coarse_hbm, fs_hbm, fr_hbm, co_hbm, cr_hbm, cv_hbm,
     ef_hbm, eb_hbm, e2_hbm, eg_hbm, nf_hbm, nb_hbm, n2_hbm, ng_hbm,
     node_out, fine_out, coarse_out,
-    L, ohT, CL, coh, crh, cohT, R, Wsr, W2, Nf, N2, H, halo, T, agg, pc, pn,
+    L, ohT, CL, coh, crh, cohT, R, Wsr, W2, Nf, N2, H, halo, T, agg, pc, ps, pn,
     fs, fr, co, cr, cv, eb, eg, nb, ng,
     lsem, fsem, osem, ssem, rsem,
     *, comm,
@@ -82,19 +83,15 @@
         rows = pl.ds(pl.multiple_of(i * CHUNK, CHUNK), CHUNK)
         return pltpu.make_async_copy(fine_hbm.at[rows], L.at[rows, pl.ds(0, D)], fsem.at[i])
 
-    def fine_store(i):
-        rows = pl.ds(pl.multiple_of(i * CHUNK, CHUNK), CHUNK)
-        return pltpu.make_async_copy(L.at[rows, pl.ds(0, D)], fine_out.at[rows], fsem.at[CHUNKS + i])
-
     def start_loads():
-        for name, _, _ in plan[:6]:
+        for name, _, _ in [*plan[:6], *plan[8:11]]:
             loads[name].start()
         fine_load(0).start()
         loads["w2"].start()
         loads["eg"].start()
         for i in range(1, CHUNKS):
             fine_load(i).start()
-        for name, _, _ in plan[8:]:
+        for name, _, _ in plan[11:]:
             loads[name].start()
 
     if comm:
@@ -272,6 +269,13 @@
         R[l, D + PAD : D + TABLE] = (mm(latent, Wsr[l, D : 2 * D]) + eb[pl.ds(l, 1), :]).astype(BF16)
         agg[...] = jnp.zeros_like(agg)
         step1(l, 0)
+
+        @pl.when(l == 0)
+        def _():
+            for name in ("co", "cr", "cv"):
+                loads[name].wait()
+            lax.fori_loop(0, CE // 128, build_coarse, 0)
+
         step1(l, 1)
         wait_halos(l)
         ends = mm(halo[l], Wsr[l, 0:D]).astype(BF16)
@@ -293,7 +297,8 @@
 
             @pl.when(l == LAYERS - 1)
             def _():
-                fine_store(i).start()
+                rows = pl.ds(pl.multiple_of(i * CHUNK, CHUNK), CHUNK)
+                fine_out[rows, :] = L[rows, 0:D]
 
             return inner
 
@@ -302,73 +307,69 @@
 
         @pl.when(l == 0)
         def _():
-            for name in ("co", "cr", "cv", "nf", "nb", "coarse", "n2", "ng", "wsr1", "r1"):
+            for name in ("nf", "nb", "coarse", "n2", "ng", "wsr1", "r1"):
                 loads[name].wait()
-            lax.fori_loop(0, CE // 128, build_coarse, 0)
 
         pc[...] = mm(CL[...], R[l, 0:D]) + mm(crh[...], R[l, D + PAD : D + PAD + 128])
         pn[...] = mm(latent, Nf[l, 0:D]) + nb[pl.ds(l, 1), :]
         node_rows(l, COARSE, NODE - COARSE, agg[COARSE:NODE])
         mine = pl.ds(pl.multiple_of(c * 1024, 1024), 1024)
         other = pl.ds(pl.multiple_of((1 - c) * 1024, 1024), 1024)
-        sender = mm(coh[:, mine], T[l, mine])
+
+        def first_half(k, inner):
+            rows = pl.ds(pl.multiple_of(k * 256, 256), 256)
+            ps[rows, :] = mm(coh[rows, mine], T[l, mine])
+            return inner
+
+        lax.fori_loop(0, CE // 256, first_half, 0)
         finish(l)
-        sender = (sender + mm(coh[:, other], T[l, other])).astype(BF16)
-        hidden = silu_half(pc[...] + mm(sender, Wsr[l, 0:D]))
-        message = norm_rows(mm(hidden, W2[l]), eg[pl.ds(l, 1), :]).astype(BF16)
-        node_rows(l, 0, COARSE, agg[0:COARSE] + mm(cohT[...], message))
+        received = agg[0:COARSE]
+        messages = []
+        for start in range(0, CE, COARSE_CHUNK):
+            rows = slice(start, start + COARSE_CHUNK)
+            sender = (ps[rows] + mm(coh[rows, other], T[l, other])).astype(BF16)
+            hidden = silu_half(pc[rows] + mm(sender, Wsr[l, 0:D]))
+            message = norm_rows(mm(hidden, W2[l]), eg[pl.ds(l, 1), :]).astype(BF16)
+            received = received + mm(cohT[:, rows], message)
+            messages.append(message)
+        node_rows(l, 0, COARSE, received)
 
         @pl.when(l < LAYERS - 1)
         def _():
             begin(l + 1, H.at[l + 1])
 
-        CL[...] += message
+        for k, message in enumerate(messages):
+            CL[k * COARSE_CHUNK : (k + 1) * COARSE_CHUNK] += message
         drain(l)
         return carry
 
     lax.fori_loop(0, LAYERS, layer, 0)
-    finals = [
-        pltpu.make_async_copy(CL, coarse_out, osem.at[0]),
-        pltpu.make_async_copy(H.at[LAYERS], node_out, osem.at[1]),
+    node_out[...] = H[LAYERS]
+    coarse_out[...] = CL[...]
+
+
+def hand_over(node, fine, coarse, node_out, fine_out, coarse_out, sem):
+    copies = [
+        pltpu.make_async_copy(src, dst, sem.at[k])
+        for k, (src, dst) in enumerate(((fine, fine_out), (coarse, coarse_out), (node, node_out)))
     ]
-    for copy in finals:
+    for copy in copies:
         copy.start()
-    for i in range(CHUNKS):
-        fine_store(i).wait()
-    for copy in finals:
-        copy.wait()
-
-
-def hand_over(node, fine, coarse, node_out, fine_out, coarse_out, N, F, C, sem):
-    pieces = [(coarse, C, coarse_out, 0, CE), (node, N, node_out, 0, NODE)]
-    pieces += [(fine, F, fine_out, k * 512, 512) for k in range(FINE // 512)]
-    arrive, leave = [], []
-    for k, (src, buffer, dst, start, count) in enumerate(pieces):
-        rows = pl.ds(start, count)
-        arrive.append(pltpu.make_async_copy(src.at[rows], buffer.at[rows], sem.at[0, k]))
-        leave.append(pltpu.make_async_copy(buffer.at[rows], dst.at[rows], sem.at[1, k]))
-        arrive[k].start()
-    for k in range(len(pieces)):
-        arrive[k].wait()
-        leave[k].start()
-    for copy in leave:
+    for copy in copies:
         copy.wait()
 
 
 def call(comm, *args):
     (node, fine, coarse, fs, fr, co, cr, cv, ef, eb, e2, eg, nf, nb, n2, ng) = args
-    anyspec = pl.BlockSpec(memory_space=pl.ANY)
+    hbm = pl.BlockSpec(memory_space=pltpu.HBM)
+    vmem = pl.BlockSpec(memory_space=pltpu.VMEM)
     copies = 9
     results = pl.pallas_call(
         functools.partial(kernel, comm=comm),
         name="processor",
-        out_shape=(
-            jax.ShapeDtypeStruct((NODE, D), BF16),
-            jax.ShapeDtypeStruct((FINE, D), BF16),
-            jax.ShapeDtypeStruct((CE, D), BF16),
-        ),
-        in_specs=[anyspec] * 16,
-        out_specs=(anyspec, anyspec, anyspec),
+        out_shape=tuple(pltpu.VMEM((n, D), BF16) for n in (NODE, FINE, CE)),
+        in_specs=[hbm] * 16,
+        out_specs=(vmem,) * 3,
         scratch_shapes=[
             pltpu.VMEM((FINE, D + TABLE), BF16),
             pltpu.VMEM((NODE, FINE), BF16),
@@ -386,6 +387,7 @@
             pltpu.VMEM((LAYERS, GATHERED, D), BF16),
             pltpu.VMEM((NODE, D), F32),
             pltpu.VMEM((CE, D), F32),
+            pltpu.VMEM((CE, D), F32),
             pltpu.VMEM((NODE, D), F32),
             pltpu.VMEM((FINE // 128, 128), jnp.int32),
             pltpu.VMEM((FINE // 128, 128), jnp.int32),
@@ -397,7 +399,7 @@
             pltpu.VMEM((LAYERS, D), F32),
             pltpu.VMEM((LAYERS, D), F32),
             pltpu.SemaphoreType.DMA((18,)),
-            pltpu.SemaphoreType.DMA((2 * CHUNKS,)),
+            pltpu.SemaphoreType.DMA((CHUNKS,)),
             pltpu.SemaphoreType.DMA((6,)),
             pltpu.SemaphoreType.DMA((LAYERS, copies)),
             pltpu.SemaphoreType.DMA((LAYERS, copies)),
@@ -411,15 +413,16 @@
         co.reshape(CE // 128, 128), cr.reshape(CE // 128, 128), cv.reshape(CE // 128, 128),
         ef, eb, e2, eg, nf, nb, n2, ng,
     )
+    anywhere = pl.BlockSpec(memory_space=pl.ANY)
     return pl.pallas_call(
         hand_over,
         name="hand_over",
         out_shape=tuple(jax.ShapeDtypeStruct((n, D), BF16) for n in (NODE, FINE, CE)),
-        in_specs=[anyspec] * 3,
-        out_specs=(anyspec,) * 3,
-        scratch_shapes=[pltpu.VMEM((n, D), BF16) for n in (NODE, FINE, CE)] + [pltpu.SemaphoreType.DMA((2, 6))],
+        in_specs=[anywhere] * 3,
+        out_specs=(hbm,) * 3,
+        scratch_shapes=[pltpu.SemaphoreType.DMA((3,))],
+        compiler_params=pltpu.CompilerParams(vmem_limit_bytes=1024 * 1024),
     )(*results)
-
 
 def solution(mesh):
     rows = P(("group", "patch"), None)

time: 50.6 us -> 45.8 us (0.905)
  Pallas kernels: 49.8 us -> 45.1 us
    pallas_call x1, Pallas kernels: 47.1 us -> 43.5 us  [call(): pl.pallas_call(functools.partial(kernel, comm=comm), name='processor', ou...]
    pallas_call x1, Pallas kernels: 2.74 us -> 1.62 us  [call(): pl.pallas_call(hand_over, name='hand_over', out_shape=tuple((jax.ShapeDty...]
where the time goes in v4:
time: 45.8 us; the launch traced here: 45.7 us
  Pallas kernels  45.1 us (98%)
  between operations  0.65 us (1%)
    pallas_call x1, Pallas kernels, call(): pl.pallas_call(functools.partial(kernel, comm=comm), name='processor', ou...  43.5 us
    pallas_call x1, Pallas kernels, call(): pl.pallas_call(hand_over, name='hand_over', out_shape=tuple((jax.ShapeDty...  1.62 us

profile of v4, /device:TPU:1, one launch (start us, length us, event | category | flops | bytes accessed | tf_op | source)
XLA Modules:
  0.0 45.7 jit_solution(15433053915748200617)
XLA Ops:
  0.6 43.5 %processor.1 = (bf16[320,512]{1,0:T(8,128)(2,1)S(1)}, bf16[2048,512]{1,0:T(8,128)(2,1)S(1)}, bf16[512,512]{1,0:T(8,128)(2,1)S(1)}) custom-call(bf16[320,512]{1,0:T(8,128)(2,1)} %h_hbm.1, bf16[2048,512]{1,0:T(8,128)(2,1)} %fine_hbm.1, bf16[512,512]{1,0:T(8,128)(2,1)} %coarse_hbm.1, s32[16,128]{1,0:T(8,128)} %bitcast.5, s32[16,128]{1,0:T(8,128)} %bitcast.6, ...), custom_call_target="tpu_custom_call" | custom-call | tf_op jit(solution)/shard_map/processor/pallas_call | solution.py:367
  44.1 1.6 %hand_over.1 = (bf16[320,512]{1,0:T(8,128)(2,1)}, bf16[2048,512]{1,0:T(8,128)(2,1)}, bf16[512,512]{1,0:T(8,128)(2,1)}) custom-call(bf16[320,512]{1,0:T(8,128)(2,1)S(1)} %get-tuple-element.6.node, bf16[2048,512]{1,0:T(8,128)(2,1)S(1)} %get-tuple-element.7.fine, bf16[512,512]{1,0:T(8,128)(2,1)S(1)} %get-tuple-element.8.coarse), custom_call_target="tpu_custom_call" | custom-call | tf_op jit(solution)/shard_map/hand_over/pallas_call | solution.py:417

commit v5 on v4

--- a/solution.py
+++ b/solution.py
@@ -34,8 +34,12 @@
     return u + u * jnp.tanh(u)
 
 
-def norm_rows(values, gain_row):
-    centred = values - jnp.mean(values, axis=-1, keepdims=True)
+def centre(ref, l):
+    weights = ref[l].astype(F32)
+    ref[l] = (weights - jnp.mean(weights, axis=-1, keepdims=True)).astype(BF16)
+
+
+def norm_rows(centred, gain_row):
     variance = jnp.mean(centred * centred, axis=-1, keepdims=True)
     return centred * lax.rsqrt(variance + EPSILON) * gain_row
 
@@ -84,14 +88,11 @@
         return pltpu.make_async_copy(fine_hbm.at[rows], L.at[rows, pl.ds(0, D)], fsem.at[i])
 
     def start_loads():
-        for name, _, _ in [*plan[:6], *plan[8:11]]:
+        for name in ("fs", "fr", "h", "wsr0", "eb", "r0", "co", "cr", "cv", "coarse", "nf", "nb", "w2", "eg"):
             loads[name].start()
-        fine_load(0).start()
-        loads["w2"].start()
-        loads["eg"].start()
-        for i in range(1, CHUNKS):
+        for i in range(CHUNKS):
             fine_load(i).start()
-        for name, _, _ in plan[11:]:
+        for name in ("n2", "ng", "wsr1", "r1"):
             loads[name].start()
 
     if comm:
@@ -136,7 +137,7 @@
 
         def remote(l, k, src, dst, target):
             return pltpu.make_async_remote_copy(
-                src_ref=src, dst_ref=dst, send_sem=ssem.at[l, k], recv_sem=rsem.at[l, k],
+                src_ref=src, dst_ref=dst, send_sem=ssem.at[l, (0, 1, 2, 2, 2, 2, 3)[k]], recv_sem=rsem.at[l, k],
                 device_id=target, device_id_type=pl.DeviceIdType.MESH,
             )
 
@@ -155,7 +156,7 @@
             return source.at[pl.ds(side * 8, 8)], dst
 
         def exchange(l):
-            return same(l, 8, c * 1024, 1024, partner)
+            return same(l, 6, c * 1024, 1024, partner)
 
         barrier = pltpu.get_barrier_semaphore()
         peers = [*second[0], *second[1], partner, following, previous]
@@ -168,32 +169,28 @@
                     for target in first[side][k]:
                         remote(l, 2 + k, *own(l, side, source), target).start()
             for side in range(2):
-                pltpu.make_async_copy(*own(l, side, source), osem.at[2 + 2 * l + side]).start()
+                pltpu.make_async_copy(*own(l, side, source), osem.at[l]).start()
             for copy in halos(l, source):
                 copy.start()
 
         def step1(l, k):
             same(l, 2 + k, 0, 2 * len(stages[k]) * 8, partner).wait_recv()
             if k == 0:
-                for side in range(2):
-                    pltpu.make_async_copy(*own(l, side, H.at[l]), osem.at[2 + 2 * l + side]).wait()
+                pltpu.make_async_copy(H.at[l, pl.ds(0, COARSE)], T.at[l, pl.ds(0, COARSE)], osem.at[l]).wait()
             start, count = pieces[k]
             for t in range(7):
                 for side in range(2):
-                    same(l, 5 + k, bundle(side) + start, count, second[side][t]).start()
+                    same(l, 5, bundle(side) + start, count, second[side][t]).start()
 
         def step2(l):
-            for k in range(3):
-                same(l, 5 + k, 0, 14 * pieces[k][1], partner).wait_recv()
+            same(l, 5, 0, 14 * 64, partner).wait_recv()
             exchange(l).start()
 
         def finish(l):
             exchange(l).wait_recv()
 
         def drain(l):
-            for k in range(3):
-                same(l, 2 + k, 0, 2 * len(stages[k]) * 8, partner).wait_send()
-                same(l, 5 + k, 0, 14 * pieces[k][1], partner).wait_send()
+            same(l, 2, 0, 14 * 8 + 14 * 64, partner).wait_send()
             for copy in [*halos(l, H.at[l]), exchange(l)]:
                 copy.wait_send()
 
@@ -240,10 +237,10 @@
         cohT[:, rows] = onehot(lax.broadcasted_iota(jnp.int32, (COARSE, 128), 0) == receiver_row)
         return carry
 
-    start_loads()
     if comm:
         pl.semaphore_wait(barrier, len(peers))
     begin(0, h_hbm)
+    start_loads()
     for name in ("fs", "fr"):
         loads[name].wait()
     lax.fori_loop(0, FINE // 128, build_fine, 0)
@@ -272,10 +269,12 @@
 
         @pl.when(l == 0)
         def _():
-            for name in ("co", "cr", "cv"):
+            for name in ("r0", "co", "cr", "cv", "coarse", "nf", "nb"):
                 loads[name].wait()
             lax.fori_loop(0, CE // 128, build_coarse, 0)
 
+        pc[...] = mm(CL[...], R[l, 0:D]) + mm(crh[...], R[l, D + PAD : D + PAD + 128])
+        pn[...] = mm(latent, Nf[l, 0:D]) + nb[pl.ds(l, 1), :]
         step1(l, 1)
         wait_halos(l)
         ends = mm(halo[l], Wsr[l, 0:D]).astype(BF16)
@@ -285,8 +284,10 @@
 
         @pl.when(l == 0)
         def _():
-            for name in ("r0", "w2", "eg"):
+            for name in ("w2", "eg"):
                 loads[name].wait()
+
+        centre(W2, l)
 
         def chunk_step(i, inner):
             @pl.when(l == 0)
@@ -303,16 +304,15 @@
             return inner
 
         lax.fori_loop(0, CHUNKS, chunk_step, 0)
-        step2(l)
 
         @pl.when(l == 0)
         def _():
-            for name in ("nf", "nb", "coarse", "n2", "ng", "wsr1", "r1"):
+            for name in ("n2", "ng", "wsr1", "r1"):
                 loads[name].wait()
 
-        pc[...] = mm(CL[...], R[l, 0:D]) + mm(crh[...], R[l, D + PAD : D + PAD + 128])
-        pn[...] = mm(latent, Nf[l, 0:D]) + nb[pl.ds(l, 1), :]
+        centre(N2, l)
         node_rows(l, COARSE, NODE - COARSE, agg[COARSE:NODE])
+        step2(l)
         mine = pl.ds(pl.multiple_of(c * 1024, 1024), 1024)
         other = pl.ds(pl.multiple_of((1 - c) * 1024, 1024), 1024)
 
@@ -363,7 +363,6 @@
     (node, fine, coarse, fs, fr, co, cr, cv, ef, eb, e2, eg, nf, nb, n2, ng) = args
     hbm = pl.BlockSpec(memory_space=pltpu.HBM)
     vmem = pl.BlockSpec(memory_space=pltpu.VMEM)
-    copies = 9
     results = pl.pallas_call(
         functools.partial(kernel, comm=comm),
         name="processor",
@@ -400,9 +399,9 @@
             pltpu.VMEM((LAYERS, D), F32),
             pltpu.SemaphoreType.DMA((18,)),
             pltpu.SemaphoreType.DMA((CHUNKS,)),
-            pltpu.SemaphoreType.DMA((6,)),
-            pltpu.SemaphoreType.DMA((LAYERS, copies)),
-            pltpu.SemaphoreType.DMA((LAYERS, copies)),
+            pltpu.SemaphoreType.DMA((LAYERS,)),
+            pltpu.SemaphoreType.DMA((LAYERS, 4)),
+            pltpu.SemaphoreType.DMA((LAYERS, 7)),
         ],
         compiler_params=pltpu.CompilerParams(
             collective_id=0 if comm else None, has_side_effects=True, vmem_limit_bytes=56 * 1024 * 1024

time: 45.8 us -> 44.9 us (0.980)
  Pallas kernels: 45.1 us -> 44.2 us
    pallas_call x1, Pallas kernels: 43.5 us -> 42.5 us  [call(): pl.pallas_call(functools.partial(kernel, comm=comm), name='processor', ou...]
where the time goes in v5:
time: 44.9 us; the launch traced here: 44.8 us
  Pallas kernels  44.2 us (98%)
  between operations  0.65 us (1%)
    pallas_call x1, Pallas kernels, call(): pl.pallas_call(functools.partial(kernel, comm=comm), name='processor', ou...  42.5 us
    pallas_call x1, Pallas kernels, call(): pl.pallas_call(hand_over, name='hand_over', out_shape=tuple((jax.ShapeDty...  1.62 us

profile of v5, /device:TPU:1, one launch (start us, length us, event | category | flops | bytes accessed | tf_op | source)
XLA Modules:
  0.0 44.8 jit_solution(5612397952929021649)
XLA Ops:
  0.6 42.5 %processor.1 = (bf16[320,512]{1,0:T(8,128)(2,1)S(1)}, bf16[2048,512]{1,0:T(8,128)(2,1)S(1)}, bf16[512,512]{1,0:T(8,128)(2,1)S(1)}) custom-call(bf16[320,512]{1,0:T(8,128)(2,1)} %h_hbm.1, bf16[2048,512]{1,0:T(8,128)(2,1)} %fine_hbm.1, bf16[512,512]{1,0:T(8,128)(2,1)} %coarse_hbm.1, s32[16,128]{1,0:T(8,128)} %bitcast.5, s32[16,128]{1,0:T(8,128)} %bitcast.6, ...), custom_call_target="tpu_custom_call" | custom-call | tf_op jit(solution)/shard_map/processor/pallas_call | solution.py:366
  43.2 1.6 %hand_over.1 = (bf16[320,512]{1,0:T(8,128)(2,1)}, bf16[2048,512]{1,0:T(8,128)(2,1)}, bf16[512,512]{1,0:T(8,128)(2,1)}) custom-call(bf16[320,512]{1,0:T(8,128)(2,1)S(1)} %get-tuple-element.6.node, bf16[2048,512]{1,0:T(8,128)(2,1)S(1)} %get-tuple-element.7.fine, bf16[512,512]{1,0:T(8,128)(2,1)S(1)} %get-tuple-element.8.coarse), custom_call_target="tpu_custom_call" | custom-call | tf_op jit(solution)/shard_map/hand_over/pallas_call | solution.py:416

commit v6 on v5

--- a/solution.py
+++ b/solution.py
@@ -276,11 +276,11 @@
         pc[...] = mm(CL[...], R[l, 0:D]) + mm(crh[...], R[l, D + PAD : D + PAD + 128])
         pn[...] = mm(latent, Nf[l, 0:D]) + nb[pl.ds(l, 1), :]
         step1(l, 1)
+        step1(l, 2)
         wait_halos(l)
         ends = mm(halo[l], Wsr[l, 0:D]).astype(BF16)
         R[l, D : D + HALO] = ends[0:HALO]
         R[l, D + HALO + NODE : D + PAD] = ends[HALO : 2 * HALO]
-        step1(l, 2)
 
         @pl.when(l == 0)
         def _():

time: 44.9 us -> 44.8 us (level)
  no operation moved by 1% of the time
where the time goes in v6:
time: 44.8 us; the launch traced here: 44.7 us
  Pallas kernels  44 us (98%)
  between operations  0.65 us (1%)
    pallas_call x1, Pallas kernels, call(): pl.pallas_call(functools.partial(kernel, comm=comm), name='processor', ou...  42.4 us
    pallas_call x1, Pallas kernels, call(): pl.pallas_call(hand_over, name='hand_over', out_shape=tuple((jax.ShapeDty...  1.62 us

profile of v6, /device:TPU:1, one launch (start us, length us, event | category | flops | bytes accessed | tf_op | source)
XLA Modules:
  0.0 44.7 jit_solution(7064094496232628509)
XLA Ops:
  0.6 42.4 %processor.1 = (bf16[320,512]{1,0:T(8,128)(2,1)S(1)}, bf16[2048,512]{1,0:T(8,128)(2,1)S(1)}, bf16[512,512]{1,0:T(8,128)(2,1)S(1)}) custom-call(bf16[320,512]{1,0:T(8,128)(2,1)} %h_hbm.1, bf16[2048,512]{1,0:T(8,128)(2,1)} %fine_hbm.1, bf16[512,512]{1,0:T(8,128)(2,1)} %coarse_hbm.1, s32[16,128]{1,0:T(8,128)} %bitcast.5, s32[16,128]{1,0:T(8,128)} %bitcast.6, ...), custom_call_target="tpu_custom_call" | custom-call | tf_op jit(solution)/shard_map/processor/pallas_call | solution.py:366
  43.1 1.6 %hand_over.1 = (bf16[320,512]{1,0:T(8,128)(2,1)}, bf16[2048,512]{1,0:T(8,128)(2,1)}, bf16[512,512]{1,0:T(8,128)(2,1)}) custom-call(bf16[320,512]{1,0:T(8,128)(2,1)S(1)} %get-tuple-element.6.node, bf16[2048,512]{1,0:T(8,128)(2,1)S(1)} %get-tuple-element.7.fine, bf16[512,512]{1,0:T(8,128)(2,1)S(1)} %get-tuple-element.8.coarse), custom_call_target="tpu_custom_call" | custom-call | tf_op jit(solution)/shard_map/hand_over/pallas_call | solution.py:416
